TPU v7x, 32 devices: a whole 2x2x4 slice. The times are simulated.
32 devices in a mesh: rows: 4 (over y, x), cols: 8 (over z, core).
Axes of the slice: x: 2, y: 2, z: 4, core: 2. Of those that a mesh axis runs over, the one named last changes fastest.
Arguments:
- pixels: bfloat16 [128, 256, 768], P('rows', 'cols'), may hold values from -6 to 6
- tissue: int32 [128, 256], P('rows', 'cols'), may hold values 0 or 1
- patch_weight: bfloat16 [768, 1024], replicated, may hold values from -0.21875 to 0.21875
- conv_weight: bfloat16 [9, 32, 1024], replicated, may hold values from -0.375 to 0.375
- kv_weight: bfloat16 [1024, 2048], replicated, may hold values from -0.1875 to 0.1875
- query_weight: bfloat16 [1024, 1024], replicated, may hold values from -0.1875 to 0.1875
- out_weight: bfloat16 [1024, 1024], replicated, may hold values from -0.1875 to 0.1875
- latents: bfloat16 [512, 1024], replicated, may hold values from -240 to 240
Outputs:
- features: bfloat16 [128, 256, 1024], P('rows', 'cols')
- latents_out: bfloat16 [512, 1024], P(('rows', 'cols'))
Inputs may be any that keep to these rules, and one draw needn't show every extreme that they name: 1 marks a patch tile that holds tissue, and at least one tile of the slab holds tissue.
All inputs are finite; a program needn't handle non-finite values. No bound on the sum of `tissue` on one device may be relied on, other than what follows from the above.
Results may differ from a plain program's by a relative error of at most 0.03.
Values may be sent and summed in bfloat16 or wider, within the bound.
A program may use at most 128 MiB of HBM per device.

v0:
```python
import functools

import jax
import jax.numpy as jnp
from jax import lax
from jax.experimental import pallas as pl
from jax.experimental.pallas import tpu as pltpu
from jax.sharding import PartitionSpec as P

HEADS = 16
BLOCK = 256
LANES = 128
PAD = 8
CORNER = 16
F32 = jnp.float32
BF16 = jnp.bfloat16
LOW = -1e30
MESH = pl.DeviceIdType.MESH


def dot(a, b):
    return jnp.dot(a, b, preferred_element_type=F32)


def core(
    tile_rows, tile_cols, heads,
    top_ref, bottom_ref, left_ref, right_ref, live_ref,
    main_hbm, patch_hbm, conv_hbm, query_hbm, kv_hbm,
    part_ref, stat_ref, features_hbm,
    main_ref, patch_ref, conv_ref, query_ref, kv_ref,
    wide_ref, taps_ref, summed_ref, keys_ref, features_ref, load_sem,
):
    loads = [
        pltpu.make_async_copy(source, target, load_sem.at[number])
        for number, (source, target) in enumerate(
            (
                (main_hbm, main_ref), (patch_hbm, patch_ref), (conv_hbm, conv_ref),
                (query_hbm, query_ref), (kv_hbm, kv_ref),
            )
        )
    ]
    for load in loads:
        load.start()
    tokens = tile_rows * tile_cols
    channels = patch_ref.shape[1]
    group = conv_ref.shape[1]
    rows_ext = tile_rows + 2
    col_ext = tile_cols + PAD
    same = (
        lax.broadcasted_iota(jnp.int32, (BLOCK, BLOCK), 0) // group
        == lax.broadcasted_iota(jnp.int32, (BLOCK, BLOCK), 1) // group
    )
    side_slot = lax.broadcasted_iota(jnp.int32, (rows_ext, PAD, BLOCK), 1)
    tall = (1, PAD, BLOCK)

    def border(values, upper, lower):
        return (
            jnp.broadcast_to(values[upper : upper + 1][:, None, :], tall),
            jnp.broadcast_to(values[:tile_rows][:, None, :], (tile_rows, PAD, BLOCK)),
            jnp.broadcast_to(values[lower : lower + 1][:, None, :], tall),
        )

    for load in loads[:3]:
        load.wait()
    for block in range(channels // BLOCK):
        lanes = slice(block * BLOCK, (block + 1) * BLOCK)
        patch = patch_ref[:, lanes]
        inner = jnp.concatenate(
            [dot(top_ref[...], patch), dot(main_ref[...], patch), dot(bottom_ref[...], patch)], 0
        )
        upper, middle, lower = border(
            dot(left_ref[...], patch), tile_rows + CORNER - 1, tile_rows + 2 * CORNER - 1
        )
        from_left = jnp.concatenate([middle, lower, upper], 0)
        upper, middle, lower = border(
            dot(right_ref[...], patch), tile_rows, tile_rows + CORNER
        )
        from_right = jnp.concatenate([upper, middle, lower], 0)
        side = jnp.where(side_slot == PAD - 1, from_left, from_right)
        full = jnp.concatenate(
            [inner.reshape(rows_ext, tile_cols, BLOCK), side], 1
        ).reshape(rows_ext * col_ext, BLOCK)
        for col_shift, amount in ((0, 1), (2, rows_ext * col_ext - 1)):
            moved = pltpu.roll(full, amount, 0).reshape(rows_ext, col_ext, BLOCK)
            moved = moved[:, :tile_cols].reshape(rows_ext * tile_cols, BLOCK)
            wide_ref[:, col_shift * BLOCK : (col_shift + 1) * BLOCK] = moved.astype(BF16)
        wide_ref[:, BLOCK : 2 * BLOCK] = inner.astype(BF16)
        for tap in range(9):
            small = conv_ref[tap, :, lanes]
            tiled = jnp.concatenate([small] * (BLOCK // group), 0)
            row_shift, col_shift = tap // 3, tap % 3
            taps_ref[row_shift, col_shift * BLOCK : (col_shift + 1) * BLOCK, :] = jnp.where(
                same, tiled, jnp.zeros_like(tiled)
            )
        total = wide_ref[tile_cols : tile_cols + tokens, BLOCK : 2 * BLOCK].astype(F32)
        for row_shift in range(3):
            first = row_shift * tile_cols
            total = total + dot(wide_ref[first : first + tokens, :], taps_ref[row_shift])
        summed_ref[:, lanes] = total

    chunk = 128
    inverse = 1.0 / channels

    def normalise(step, _):
        at = pl.ds(pl.multiple_of(step * chunk, chunk), chunk)
        values = summed_ref[at, :]
        centred = values - jnp.sum(values, axis=-1, keepdims=True) * inverse
        variance = jnp.sum(centred * centred, axis=-1, keepdims=True) * inverse
        features_ref[at, :] = (centred * lax.rsqrt(variance + 1e-05)).astype(BF16)
        return 0

    lax.fori_loop(0, tokens // chunk, normalise, 0)
    store = pltpu.make_async_copy(features_ref, features_hbm, load_sem.at[len(loads)])
    store.start()
    head_dim = channels // heads
    for load in loads[3:]:
        load.wait()

    def project(step, _):
        at = pl.ds(pl.multiple_of(step * BLOCK, BLOCK), BLOCK)
        keys_ref[:, at] = dot(features_ref[...], kv_ref[:, at]).astype(BF16)
        return 0

    lax.fori_loop(0, keys_ref.shape[1] // BLOCK, project, 0)

    latent_count = query_ref.shape[0]
    token_lane = lax.broadcasted_iota(jnp.int32, (tokens, LANES), 1)
    query_lane = lax.broadcasted_iota(jnp.int32, (latent_count, LANES), 1)
    token_low = token_lane < head_dim
    query_low = query_lane < head_dim
    stat_ref[...] = jnp.zeros_like(stat_ref)

    def attend(pair, _):
        at = pl.ds(pl.multiple_of(pair * LANES, LANES), LANES)
        value_at = pl.ds(pl.multiple_of(channels + pair * LANES, LANES), LANES)
        queries = query_ref[:, at]
        keys = keys_ref[:, at]
        values = keys_ref[:, value_at]
        live = live_ref[...]
        bias = (live - 1.0) * (-LOW)
        bias = bias.astype(BF16)
        ones = jnp.ones_like(values)
        results = []
        stats = stat_ref[...]
        for which in range(2):
            query_mine = query_low if which == 0 else jnp.logical_not(query_low)
            token_mine = token_low if which == 0 else jnp.logical_not(token_low)
            spot = head_dim if which == 0 else 0
            marker = (query_lane == spot).astype(F32).astype(BF16)
            query_head = jnp.where(query_mine, queries, marker)
            key_head = jnp.where(token_mine, keys, bias)
            value_head = jnp.where(token_mine, values, ones) * live
            scores = lax.dot_general(
                query_head, key_head, (((1,), (1,)), ((), ())), preferred_element_type=F32
            )
            peak = jnp.max(scores, axis=1, keepdims=True)
            weights = jnp.exp(scores - peak).astype(BF16)
            got = dot(weights, value_head)
            results.append(got)
            head = pair * 2 + which
            total = got[:, spot : spot + 1]
            stats = jnp.where(query_lane == head, peak, stats)
            stats = jnp.where(query_lane == head_dim + head, total, stats)
        stat_ref[...] = stats
        numer = jnp.where(query_low, results[0], results[1])
        denom = jnp.where(query_low, results[1], results[0])
        denom = pltpu.roll(denom, head_dim, 1)
        part_ref[:, at] = jnp.where(denom > 0, numer / jnp.maximum(denom, 1e-30), 0.0).astype(BF16)
        return 0

    lax.fori_loop(0, heads // 2, attend, 0)
    store.wait()


def local_work(borders, queries, live, pixels, patch_weight, conv_weight, kv_weight):
    tile_rows, tile_cols, patch_in = pixels.shape
    channels = patch_weight.shape[1]
    tokens = tile_rows * tile_cols
    latent_count = queries.shape[0]
    rows_ext = tile_rows + 2
    vmem = pl.BlockSpec(memory_space=pltpu.VMEM)
    leave = pl.BlockSpec(memory_space=pl.ANY)
    loaded = (
        pixels.reshape(tokens, patch_in), patch_weight, conv_weight, queries, kv_weight,
    )
    part, stat, features = pl.pallas_call(
        functools.partial(core, tile_rows, tile_cols, HEADS),
        out_shape=(
            jax.ShapeDtypeStruct((latent_count, channels), BF16),
            jax.ShapeDtypeStruct((latent_count, LANES), F32),
            jax.ShapeDtypeStruct((tokens, channels), BF16),
        ),
        in_specs=[vmem] * 5 + [leave] * len(loaded),
        out_specs=(vmem, vmem, leave),
        scratch_shapes=[pltpu.VMEM(array.shape, BF16) for array in loaded]
        + [
            pltpu.VMEM((rows_ext * tile_cols, 3 * BLOCK), BF16),
            pltpu.VMEM((3, 3 * BLOCK, BLOCK), BF16),
            pltpu.VMEM((tokens, channels), F32),
            pltpu.VMEM((tokens, 2 * channels), BF16),
            pltpu.VMEM((tokens, channels), BF16),
            pltpu.SemaphoreType.DMA((len(loaded) + 1,)),
        ],
        compiler_params=pltpu.CompilerParams(vmem_limit_bytes=60 * 1024 * 1024),
        name="local_work",
    )(*borders, live, *loaded)
    return features, part, stat


def greet(
    head_dim,
    pixels_ref, first_ref, last_ref, latent_hbm, weight_hbm,
    top_ref, bottom_ref, left_ref, right_ref, query_ref,
    latent_ref, weight_ref, send_sem, recv_sem, load_sem,
):
    loads = [
        pltpu.make_async_copy(latent_hbm, latent_ref, load_sem.at[0]),
        pltpu.make_async_copy(weight_hbm, weight_ref, load_sem.at[1]),
    ]
    for load in loads:
        load.start()
    channels = query_ref.shape[1]
    tile_rows, tile_cols, _ = pixels_ref.shape
    row_count, col_count = lax.axis_size("rows"), lax.axis_size("cols")
    row, col = lax.axis_index("rows"), lax.axis_index("cols")
    low, high = slice(0, CORNER), slice(tile_cols - CORNER, tile_cols)
    column = slice(0, tile_rows)
    above = slice(tile_rows, tile_rows + CORNER)
    below = slice(tile_rows + CORNER, tile_rows + 2 * CORNER)
    end = tile_rows - 1
    moves = (
        (1, 0, pixels_ref.at[end], top_ref),
        (-1, 0, pixels_ref.at[0], bottom_ref),
        (0, 1, last_ref, left_ref.at[column]),
        (0, -1, first_ref, right_ref.at[column]),
        (1, 1, pixels_ref.at[end, high], left_ref.at[above]),
        (1, -1, pixels_ref.at[end, low], right_ref.at[above]),
        (-1, 1, pixels_ref.at[0, high], left_ref.at[below]),
        (-1, -1, pixels_ref.at[0, low], right_ref.at[below]),
    )

    def inside(down, across):
        ok = None
        for at, step, count in ((row, down, row_count), (col, across, col_count)):
            if step:
                here = at + step < count if step > 0 else at + step >= 0
                ok = here if ok is None else jnp.logical_and(ok, here)
        return ok

    barrier = pltpu.get_barrier_semaphore()
    for down, across, _, _ in moves:
        @pl.when(inside(down, across))
        def _(down=down, across=across):
            pl.semaphore_signal(
                barrier, inc=1, device_id=(row + down, col + across), device_id_type=MESH
            )
    tall = 1 + (row > 0).astype(jnp.int32) + (row < row_count - 1).astype(jnp.int32)
    wide = 1 + (col > 0).astype(jnp.int32) + (col < col_count - 1).astype(jnp.int32)
    pl.semaphore_wait(barrier, tall * wide - 1)

    def make(number):
        down, across, source, target = moves[number]
        return pltpu.make_async_remote_copy(
            src_ref=source, dst_ref=target,
            send_sem=send_sem.at[number], recv_sem=recv_sem.at[number],
            device_id=(row + down, col + across), device_id_type=MESH,
        )

    for number, (down, across, _, _) in enumerate(moves):
        @pl.when(inside(down, across))
        def _(number=number):
            make(number).start()
    for load in loads:
        load.wait()

    def ask(step, _):
        at = pl.ds(pl.multiple_of(step * BLOCK, BLOCK), BLOCK)
        asked = dot(latent_ref[...], weight_ref[:, at]).astype(BF16).astype(F32)
        query_ref[:, at] = (asked * head_dim ** -0.5).astype(BF16)
        return 0

    lax.fori_loop(0, channels // BLOCK, ask, 0)
    for number, (down, across, _, target) in enumerate(moves):
        @pl.when(inside(-down, -across))
        def _(number=number):
            make(number).wait_recv()

        @pl.when(jnp.logical_not(inside(-down, -across)))
        def _(target=target):
            target[...] = jnp.zeros(target.shape, BF16)
    for number, (down, across, _, _) in enumerate(moves):
        @pl.when(inside(down, across))
        def _(number=number):
            make(number).wait_send()


def borders_of(pixels, latents, query_weight):
    tile_rows, tile_cols, patch_in = pixels.shape
    vmem = pl.BlockSpec(memory_space=pltpu.VMEM)
    flat = jax.ShapeDtypeStruct((tile_cols, patch_in), BF16)
    tall = jax.ShapeDtypeStruct((tile_rows + 2 * CORNER, patch_in), BF16)
    channels = query_weight.shape[1]
    leave = pl.BlockSpec(memory_space=pl.ANY)
    *borders, queries = pl.pallas_call(
        functools.partial(greet, channels // HEADS),
        out_shape=(flat, flat, tall, tall, jax.ShapeDtypeStruct((latents.shape[0], channels), BF16)),
        in_specs=[leave, vmem, vmem, leave, leave],
        out_specs=(vmem,) * 5,
        scratch_shapes=[
            pltpu.VMEM(latents.shape, BF16),
            pltpu.VMEM(query_weight.shape, BF16),
            pltpu.SemaphoreType.DMA((8,)),
            pltpu.SemaphoreType.DMA((8,)),
            pltpu.SemaphoreType.DMA((2,)),
        ],
        compiler_params=pltpu.CompilerParams(
            collective_id=2, has_side_effects=True, vmem_limit_bytes=60 * 1024 * 1024
        ),
        name="borders",
    )(pixels, pixels[:, 0], pixels[:, -1], latents, query_weight)
    return borders, queries


def spread(values, heads, head_dim, low):
    return [
        jnp.where(low, values[:, 2 * pair : 2 * pair + 1], values[:, 2 * pair + 1 : 2 * pair + 2])
        for pair in range(heads // 2)
    ]


def blend(parts, stats, heads, head_dim):
    rows = parts[0].shape[0]
    lane = lax.broadcasted_iota(jnp.int32, (rows, LANES), 1)
    low = lane < head_dim
    peaks = stats
    totals = [pltpu.roll(stat, LANES - head_dim, 1) for stat in stats]
    top = functools.reduce(jnp.maximum, peaks)
    shares = [jnp.exp(peak - top) * total for peak, total in zip(peaks, totals)]
    whole = functools.reduce(jnp.add, shares)
    inverse = jnp.where(whole > 0, 1.0 / jnp.maximum(whole, 1e-30), 0.0)
    columns = [0.0] * (heads // 2)
    for part, share in zip(parts, shares):
        factors = spread(share * inverse, heads, head_dim, low)
        for pair in range(heads // 2):
            piece = part[:, pair * LANES : (pair + 1) * LANES].astype(F32)
            columns[pair] = columns[pair] + factors[pair] * piece
    used = lane < heads
    stat = jnp.where(used, top, 0.0)
    stat = jnp.where(lane < head_dim, stat, pltpu.roll(jnp.where(used, whole, 0.0), head_dim, 1))
    return columns, stat


def exchange(
    heads,
    part_ref, stat_ref, weight_hbm,
    out_ref,
    part_one, stat_one, sum_one, tot_one, part_two, stat_two, sum_two, tot_two,
    part_three, stat_three, part_own, stat_own, weight_ref, send_sem, recv_sem, load_sem,
):
    row_count, half, _, own, channels = part_ref.shape
    head_dim = channels // heads
    row = lax.axis_index("rows")
    col = lax.axis_index("cols")
    side = lax.rem(col, 2)
    slot = lax.div(col, 2)
    mine = [
        pltpu.make_async_copy(part_ref.at[:, :, side], part_own, load_sem.at[0]),
        pltpu.make_async_copy(stat_ref.at[:, :, side], stat_own, load_sem.at[1]),
    ]
    load = pltpu.make_async_copy(weight_hbm, weight_ref, load_sem.at[2])
    for copy in mine:
        copy.start()

    twin = (row, slot * 2 + (1 - side))
    row_peers = [(lax.rem(row + step, row_count), col) for step in range(1, row_count)]
    col_peers = [(row, lax.rem(slot + step, half) * 2 + side) for step in range(1, half)]
    barrier = pltpu.get_barrier_semaphore()
    for peer in [twin] + row_peers + col_peers:
        pl.semaphore_signal(barrier, inc=1, device_id=peer, device_id_type=MESH)
    pl.semaphore_wait(barrier, 1 + len(row_peers) + len(col_peers))

    def send(source, target, peer, number):
        copy = pltpu.make_async_remote_copy(
            src_ref=source, dst_ref=target,
            send_sem=send_sem.at[number], recv_sem=recv_sem.at[number],
            device_id=peer, device_id_type=MESH,
        )
        copy.start()
        return copy

    row_order = [lax.rem(row + step, row_count) for step in range(1, row_count + 1)]
    col_order = [lax.rem(slot + step, half) for step in range(1, half + 1)]
    ones, twos, threes = [], [], []
    for step, a in enumerate(row_order):
        ones.append(
            (
                send(part_ref.at[a, :, 1 - side], part_one.at[a], twin, 2 * step),
                send(stat_ref.at[a, :, 1 - side], stat_one.at[a], twin, 2 * step + 1),
            )
        )
    load.start()
    for copy in mine:
        copy.wait()
    number = 2 * row_count
    for step, a in enumerate(row_order):
        for copy in ones[step]:
            copy.wait_recv()

        def first(b, _, a=a):
            columns, stat = blend(
                [part_own[a, b], part_one[a, b]], [stat_own[a, b], stat_one[a, b]],
                heads, head_dim,
            )
            for pair, column in enumerate(columns):
                sum_one[a, b, :, pair * LANES : (pair + 1) * LANES] = column.astype(BF16)
            tot_one[a, b] = stat
            return 0

        lax.fori_loop(0, half, first, 0)
        if step < row_count - 1:
            twos.append(send(sum_one.at[a], part_two.at[step], row_peers[step], number))
            twos.append(send(tot_one.at[a], stat_two.at[step], row_peers[step], number + 1))
            number += 2
    for copy in twos:
        copy.wait_recv()
    for step, b in enumerate(col_order):
        columns, stat = blend(
            [sum_one[row, b]] + [part_two[other, b] for other in range(row_count - 1)],
            [tot_one[row, b]] + [stat_two[other, b] for other in range(row_count - 1)],
            heads, head_dim,
        )
        if step < half - 1:
            for pair, column in enumerate(columns):
                sum_two[b, :, pair * LANES : (pair + 1) * LANES] = column.astype(BF16)
            tot_two[b] = stat
            threes.append(send(sum_two.at[b], part_three.at[step], col_peers[step], number))
            threes.append(send(tot_two.at[b], stat_three.at[step], col_peers[step], number + 1))
            number += 2
    for copy in threes:
        copy.wait_recv()
    columns, _ = blend(
        [jnp.concatenate(columns, 1)] + [part_three[step] for step in range(half - 1)],
        [stat] + [stat_three[step] for step in range(half - 1)],
        heads, head_dim,
    )
    for copy in [copy for both in ones for copy in both] + twos + threes:
        copy.wait_send()
    attended = jnp.concatenate(columns, 1)
    mean = jnp.sum(attended * attended, axis=-1, keepdims=True) * (1.0 / channels)
    normed = (attended * lax.rsqrt(mean + 1e-06)).astype(BF16)
    load.wait()
    out_ref[...] = dot(normed, weight_ref[...]).astype(BF16)


def combine(part, stat, out_weight):
    row_count, col_count = lax.axis_size("rows"), lax.axis_size("cols")
    half = col_count // 2
    latent_count, channels = part.shape
    own = latent_count // (row_count * col_count)
    part = part.reshape(row_count, half, 2, own, channels)
    stat = stat.reshape(row_count, half, 2, own, LANES)
    vmem = pl.BlockSpec(memory_space=pltpu.VMEM)
    copies = 2 * (2 * row_count - 1) + 2 * (half - 1)

    def pairs(*extent):
        return [
            pltpu.VMEM(extent + (own, channels), BF16), pltpu.VMEM(extent + (own, LANES), F32)
        ]

    return pl.pallas_call(
        functools.partial(exchange, HEADS),
        out_shape=jax.ShapeDtypeStruct((own, out_weight.shape[1]), BF16),
        in_specs=[pl.BlockSpec(memory_space=pl.ANY)] * 3,
        out_specs=vmem,
        scratch_shapes=pairs(row_count, half)
        + pairs(row_count, half)
        + pairs(row_count - 1, half)
        + pairs(half)
        + pairs(half - 1)
        + pairs(row_count, half)
        + [
            pltpu.VMEM(out_weight.shape, BF16),
            pltpu.SemaphoreType.DMA((copies,)),
            pltpu.SemaphoreType.DMA((copies,)),
            pltpu.SemaphoreType.DMA((3,)),
        ],
        compiler_params=pltpu.CompilerParams(
            collective_id=1, has_side_effects=True, vmem_limit_bytes=60 * 1024 * 1024
        ),
        name="combine",
    )(part, stat, out_weight)


def shards(pixels, tissue, patch_weight, conv_weight, kv_weight, query_weight, out_weight, latents):
    tile_rows, tile_cols, _ = pixels.shape
    channels = patch_weight.shape[1]
    tokens = tile_rows * tile_cols
    live = jnp.broadcast_to((tissue.reshape(tokens, 1) > 0).astype(BF16), (tokens, LANES))
    borders, queries = borders_of(pixels, latents, query_weight)
    features, part, stat = local_work(
        borders, queries, live, pixels, patch_weight, conv_weight, kv_weight
    )
    latents_out = combine(part, stat, out_weight)
    return (features.reshape(tile_rows, tile_cols, channels), latents_out)


def solution(mesh):
    return jax.shard_map(
        shards,
        mesh=mesh,
        in_specs=(P("rows", "cols", None), P("rows", "cols"), P(), P(), P(), P(), P(), P()),
        out_specs=(P("rows", "cols", None), P(("rows", "cols"), None)),
        check_vma=False,
    )
```

profile of v0, /device:TPU:0, one launch (start us, length us, event | category | flops | bytes accessed | tf_op | source)
XLA Modules:
  0.0 76.6 jit_solution(6655193306085128594)
XLA Ops:
  0.6 0.7 compare_convert_fusion
  1.4 0.1 reshape.34
  1.4 1.3 %fusion = (bf16[32,1,768]{2,1,0:T(2,128)(2,1)S(1)}, bf16[32,1,768]{2,1,0:T(2,128)(2,1)S(1)}) fusion(bf16[32,32,768]{2,1,0:T(8,128)(2,1)} %pixels_ref.1), kind=kLoop, calls=%fused_computation.3 | loop fusion | bytes 196608 | tf_op jit(solution)/shard_map/slice | solution.py:320
  2.7 0.6 copy_bitcast_fusion
  3.4 0.9 %broadcast_in_dim.2.live_ref = bf16[1024,128]{1,0:T(8,128)(2,1)} broadcast(bf16[1024]{0:T(1024)(128)(2,1)S(1)} %reshape.34), dimensions={0} | broadcast | bytes 264192 | tf_op jit(solution)/shard_map/broadcast_in_dim | solution.py:498
  4.3 12.0 %borders.1 = (bf16[32,768]{1,0:T(8,128)(2,1)}, bf16[32,768]{1,0:T(8,128)(2,1)}, bf16[64,768]{1,0:T(8,128)(2,1)}, bf16[64,768]{1,0:T(8,128)(2,1)}, bf16[512,1024]{1,0:T(8,128)(2,1)}) custom-call(bf16[32,32,768]{2,1,0:T(8,128)(2,1)} %pixels_ref.1, bf16[32,768]{1,0:T(8,128)(2,1)} %get-tuple-element.21.first_ref, bf16[32,768]{1,0:T(8,128)(2,1)} %get-tuple-element.20.last_ref, ...), custom_call_target="tpu_custom_call" | custom-call | tf_op jit(solution)/shard_map/borders/pallas_call | solution.py:304
  16.3 36.7 %local_work.1 = (bf16[512,1024]{1,0:T(8,128)(2,1)}, f32[512,128]{1,0:T(8,128)}, bf16[1024,1024]{1,0:T(8,128)(2,1)}) custom-call(bf16[32,768]{1,0:T(8,128)(2,1)} %get-tuple-element.10.top_ref, bf16[32,768]{1,0:T(8,128)(2,1)} %get-tuple-element.11.bottom_ref, bf16[64,768]{1,0:T(8,128)(2,1)} %get-tuple-element.12.left_ref, ...), custom_call_target="tpu_custom_call" | custom-call | tf_op jit(solution)/shard_map/local_work/pallas_call | solution.py:186
  53.0 22.2 %combine.1 = bf16[16,1024]{1,0:T(8,128)(2,1)} custom-call(bf16[4,4,2,16,1024]{4,3,2,1,0:T(8,128)(2,1)} %bitcast.9, f32[4,4,2,16,128]{4,3,2,1,0:T(8,128)} %bitcast.10, bf16[1024,1024]{1,0:T(8,128)(2,1)} %weight_hbm.3), custom_call_target="tpu_custom_call" | custom-call | tf_op jit(solution)/shard_map/combine/pallas_call | solution.py:470
  75.2 1.4 %copy.17 = bf16[16,1024]{1,0:T(8,128)(2,1)} copy(bf16[16,1024]{1,0:T(8,128)(2,1)} %combine.1) | data formatting | bytes 65536
where the time goes:
time: 76.9 us; the launch traced here: 76.6 us
  Pallas kernels  70.9 us (92%)
  local copies, waits for them, and re-layouts  4.31 us (6%)
    pallas_call x1, Pallas kernels, local_work(): pl.pallas_call(functools.partial(core, tile_rows, tile_cols, HEADS), out_...  36.7 us
    pallas_call x1, Pallas kernels, combine(): pl.pallas_call(functools.partial(exchange, HEADS), out_shape=jax.ShapeDty...  22.2 us
    pallas_call x1, Pallas kernels, borders_of(): pl.pallas_call(functools.partial(greet, channels // HEADS), out_shape=(fl...  12 us

commit v1 on v0

v1 whole, which is shorter than its diff:
```python
import functools

import jax
import jax.numpy as jnp
from jax import lax
from jax.experimental import pallas as pl
from jax.experimental.pallas import tpu as pltpu
from jax.sharding import PartitionSpec as P

HEADS = 16
BLOCK = 256
LANES = 128
PAD = 8
CORNER = 16
F32 = jnp.float32
BF16 = jnp.bfloat16
LOW = -1e30
LAG = 4
LOG2_E = 1.4426950408889634
MESH = pl.DeviceIdType.MESH


def dot(a, b):
    return jnp.dot(a, b, preferred_element_type=F32)


def core(
    tile_rows, tile_cols,
    top_ref, bottom_ref, left_ref, right_ref,
    main_hbm, patch_hbm, conv_hbm, kv_hbm,
    features_hbm, keys_hbm,
    main_ref, patch_ref, conv_ref, kv_ref,
    wide_ref, taps_ref, summed_ref, keys_ref, features_ref, load_sem, key_sem,
):
    loads = [
        pltpu.make_async_copy(source, target, load_sem.at[number])
        for number, (source, target) in enumerate(
            (
                (main_hbm, main_ref), (patch_hbm, patch_ref), (conv_hbm, conv_ref),
                (kv_hbm, kv_ref),
            )
        )
    ]
    for load in loads:
        load.start()
    tokens = tile_rows * tile_cols
    channels = patch_ref.shape[1]
    group = conv_ref.shape[1]
    rows_ext = tile_rows + 2
    col_ext = tile_cols + PAD
    same = (
        lax.broadcasted_iota(jnp.int32, (BLOCK, BLOCK), 0) // group
        == lax.broadcasted_iota(jnp.int32, (BLOCK, BLOCK), 1) // group
    )
    side_slot = lax.broadcasted_iota(jnp.int32, (rows_ext, PAD, BLOCK), 1)
    tall = (1, PAD, BLOCK)

    def border(values, upper, lower):
        return (
            jnp.broadcast_to(values[upper : upper + 1][:, None, :], tall),
            jnp.broadcast_to(values[:tile_rows][:, None, :], (tile_rows, PAD, BLOCK)),
            jnp.broadcast_to(values[lower : lower + 1][:, None, :], tall),
        )

    for load in loads[:3]:
        load.wait()
    for block in range(channels // BLOCK):
        lanes = slice(block * BLOCK, (block + 1) * BLOCK)
        patch = patch_ref[:, lanes]
        inner = jnp.concatenate(
            [dot(top_ref[...], patch), dot(main_ref[...], patch), dot(bottom_ref[...], patch)], 0
        )
        upper, middle, lower = border(
            dot(left_ref[...], patch), tile_rows + CORNER - 1, tile_rows + 2 * CORNER - 1
        )
        from_left = jnp.concatenate([middle, lower, upper], 0)
        upper, middle, lower = border(
            dot(right_ref[...], patch), tile_rows, tile_rows + CORNER
        )
        from_right = jnp.concatenate([upper, middle, lower], 0)
        side = jnp.where(side_slot == PAD - 1, from_left, from_right)
        full = jnp.concatenate(
            [inner.reshape(rows_ext, tile_cols, BLOCK), side], 1
        ).reshape(rows_ext * col_ext, BLOCK)
        for col_shift, amount in ((0, 1), (2, rows_ext * col_ext - 1)):
            moved = pltpu.roll(full, amount, 0).reshape(rows_ext, col_ext, BLOCK)
            moved = moved[:, :tile_cols].reshape(rows_ext * tile_cols, BLOCK)
            wide_ref[:, col_shift * BLOCK : (col_shift + 1) * BLOCK] = moved.astype(BF16)
        wide_ref[:, BLOCK : 2 * BLOCK] = inner.astype(BF16)
        for tap in range(9):
            small = conv_ref[tap, :, lanes]
            tiled = jnp.concatenate([small] * (BLOCK // group), 0)
            row_shift, col_shift = tap // 3, tap % 3
            taps_ref[row_shift, col_shift * BLOCK : (col_shift + 1) * BLOCK, :] = jnp.where(
                same, tiled, jnp.zeros_like(tiled)
            )
        total = wide_ref[tile_cols : tile_cols + tokens, BLOCK : 2 * BLOCK].astype(F32)
        for row_shift in range(3):
            first = row_shift * tile_cols
            total = total + dot(wide_ref[first : first + tokens, :], taps_ref[row_shift])
        summed_ref[:, lanes] = total

    chunk = 128
    inverse = 1.0 / channels

    def normalise(step, _):
        at = pl.ds(pl.multiple_of(step * chunk, chunk), chunk)
        values = summed_ref[at, :]
        centred = values - jnp.sum(values, axis=-1, keepdims=True) * inverse
        variance = jnp.sum(centred * centred, axis=-1, keepdims=True) * inverse
        features_ref[at, :] = (centred * lax.rsqrt(variance + 1e-05)).astype(BF16)
        return 0

    lax.fori_loop(0, tokens // chunk, normalise, 0)
    store = pltpu.make_async_copy(features_ref, features_hbm, load_sem.at[len(loads)])
    store.start()
    loads[3].wait()

    def stored(step):
        at = pl.ds(pl.multiple_of(step * BLOCK, BLOCK), BLOCK)
        return pltpu.make_async_copy(keys_ref.at[:, at], keys_hbm.at[:, at], key_sem.at[step])

    def project(step, _):
        at = pl.ds(pl.multiple_of(step * BLOCK, BLOCK), BLOCK)
        keys_ref[:, at] = dot(features_ref[...], kv_ref[:, at]).astype(BF16)
        stored(step).start()
        return 0

    lax.fori_loop(0, keys_ref.shape[1] // BLOCK, project, 0)

    def finish(step, _):
        stored(step).wait()
        return 0

    lax.fori_loop(0, keys_ref.shape[1] // BLOCK, finish, 0)
    store.wait()


def local_work(borders, pixels, patch_weight, conv_weight, kv_weight):
    tile_rows, tile_cols, patch_in = pixels.shape
    channels = patch_weight.shape[1]
    tokens = tile_rows * tile_cols
    rows_ext = tile_rows + 2
    vmem = pl.BlockSpec(memory_space=pltpu.VMEM)
    leave = pl.BlockSpec(memory_space=pl.ANY)
    loaded = (pixels.reshape(tokens, patch_in), patch_weight, conv_weight, kv_weight)
    return pl.pallas_call(
        functools.partial(core, tile_rows, tile_cols),
        out_shape=(
            jax.ShapeDtypeStruct((tokens, channels), BF16),
            jax.ShapeDtypeStruct((tokens, 2 * channels), BF16),
        ),
        in_specs=[vmem] * 4 + [leave] * len(loaded),
        out_specs=(leave, leave),
        scratch_shapes=[pltpu.VMEM(array.shape, BF16) for array in loaded]
        + [
            pltpu.VMEM((rows_ext * tile_cols, 3 * BLOCK), BF16),
            pltpu.VMEM((3, 3 * BLOCK, BLOCK), BF16),
            pltpu.VMEM((tokens, channels), F32),
            pltpu.VMEM((tokens, 2 * channels), BF16),
            pltpu.VMEM((tokens, channels), BF16),
            pltpu.SemaphoreType.DMA((len(loaded) + 1,)),
            pltpu.SemaphoreType.DMA((2 * channels // BLOCK,)),
        ],
        compiler_params=pltpu.CompilerParams(vmem_limit_bytes=60 * 1024 * 1024),
        name="local_work",
    )(*borders, *loaded)


def greet(
    pixels_ref, first_ref, last_ref, latent_hbm, weight_hbm,
    top_ref, bottom_ref, left_ref, right_ref, query_ref,
    latent_ref, weight_ref, send_sem, recv_sem, load_sem,
):
    loads = [
        pltpu.make_async_copy(latent_hbm.at[:, :, 0], latent_ref.at[0], load_sem.at[0]),
        pltpu.make_async_copy(latent_hbm.at[:, :, 1], latent_ref.at[1], load_sem.at[1]),
        pltpu.make_async_copy(weight_hbm, weight_ref, load_sem.at[2]),
    ]
    for load in loads:
        load.start()
    channels = query_ref.shape[1]
    tile_rows, tile_cols, _ = pixels_ref.shape
    row_count, col_count = lax.axis_size("rows"), lax.axis_size("cols")
    row, col = lax.axis_index("rows"), lax.axis_index("cols")
    low, high = slice(0, CORNER), slice(tile_cols - CORNER, tile_cols)
    column = slice(0, tile_rows)
    above = slice(tile_rows, tile_rows + CORNER)
    below = slice(tile_rows + CORNER, tile_rows + 2 * CORNER)
    end = tile_rows - 1
    moves = (
        (1, 0, pixels_ref.at[end], top_ref),
        (-1, 0, pixels_ref.at[0], bottom_ref),
        (0, 1, last_ref, left_ref.at[column]),
        (0, -1, first_ref, right_ref.at[column]),
        (1, 1, pixels_ref.at[end, high], left_ref.at[above]),
        (1, -1, pixels_ref.at[end, low], right_ref.at[above]),
        (-1, 1, pixels_ref.at[0, high], left_ref.at[below]),
        (-1, -1, pixels_ref.at[0, low], right_ref.at[below]),
    )

    def inside(down, across):
        ok = None
        for at, step, count in ((row, down, row_count), (col, across, col_count)):
            if step:
                here = at + step < count if step > 0 else at + step >= 0
                ok = here if ok is None else jnp.logical_and(ok, here)
        return ok

    barrier = pltpu.get_barrier_semaphore()
    for down, across, _, _ in moves:
        @pl.when(inside(down, across))
        def _(down=down, across=across):
            pl.semaphore_signal(
                barrier, inc=1, device_id=(row + down, col + across), device_id_type=MESH
            )
    tall = 1 + (row > 0).astype(jnp.int32) + (row < row_count - 1).astype(jnp.int32)
    wide = 1 + (col > 0).astype(jnp.int32) + (col < col_count - 1).astype(jnp.int32)
    pl.semaphore_wait(barrier, tall * wide - 1)

    def make(number):
        down, across, source, target = moves[number]
        return pltpu.make_async_remote_copy(
            src_ref=source, dst_ref=target,
            send_sem=send_sem.at[number], recv_sem=recv_sem.at[number],
            device_id=(row + down, col + across), device_id_type=MESH,
        )

    for number, (down, across, _, _) in enumerate(moves):
        @pl.when(inside(down, across))
        def _(number=number):
            make(number).start()
    for load in loads:
        load.wait()

    def ask(step, _):
        at = pl.ds(pl.multiple_of(step * BLOCK, BLOCK), BLOCK)
        asked = latent_ref[...].reshape(query_ref.shape[0], weight_ref.shape[0])
        query_ref[:, at] = dot(asked, weight_ref[:, at]).astype(BF16)
        return 0

    lax.fori_loop(0, channels // BLOCK, ask, 0)
    for number, (down, across, _, target) in enumerate(moves):
        @pl.when(inside(-down, -across))
        def _(number=number):
            make(number).wait_recv()

        @pl.when(jnp.logical_not(inside(-down, -across)))
        def _(target=target):
            target[...] = jnp.zeros(target.shape, BF16)
    for number, (down, across, _, _) in enumerate(moves):
        @pl.when(inside(down, across))
        def _(number=number):
            make(number).wait_send()


def borders_of(pixels, latents, query_weight):
    tile_rows, tile_cols, patch_in = pixels.shape
    vmem = pl.BlockSpec(memory_space=pltpu.VMEM)
    flat = jax.ShapeDtypeStruct((tile_cols, patch_in), BF16)
    tall = jax.ShapeDtypeStruct((tile_rows + 2 * CORNER, patch_in), BF16)
    latent_count, channels = latents.shape[0], query_weight.shape[1]
    row_count, col_count = lax.axis_size("rows"), lax.axis_size("cols")
    own = latent_count // (row_count * col_count)
    latents = latents.reshape(row_count, col_count // 2, 2, own, latents.shape[1])
    ordered = (2, row_count, col_count // 2, own, latents.shape[-1])
    leave = pl.BlockSpec(memory_space=pl.ANY)
    *borders, queries = pl.pallas_call(
        greet,
        out_shape=(flat, flat, tall, tall, jax.ShapeDtypeStruct((latent_count, channels), BF16)),
        in_specs=[leave, vmem, vmem, leave, leave],
        out_specs=(vmem,) * 5,
        scratch_shapes=[
            pltpu.VMEM(ordered, BF16),
            pltpu.VMEM(query_weight.shape, BF16),
            pltpu.SemaphoreType.DMA((8,)),
            pltpu.SemaphoreType.DMA((8,)),
            pltpu.SemaphoreType.DMA((3,)),
        ],
        compiler_params=pltpu.CompilerParams(
            collective_id=2, has_side_effects=True, vmem_limit_bytes=60 * 1024 * 1024
        ),
        name="borders",
    )(pixels, pixels[:, 0], pixels[:, -1], latents, query_weight)
    return borders, queries


def merge(items, gain):
    top = functools.reduce(jnp.maximum, [peak for _, peak, _ in items])
    number, total = 0.0, 0.0
    for values, peak, whole in items:
        share = jnp.exp2((peak - top) * gain)
        number = number + share * values
        total = total + share * whole
    return number, top, total


def attend(
    heads,
    tissue_ref, query_hbm, keys_hbm, weight_hbm,
    out_ref,
    query_ref, keys_ref, values_ref, weight_ref, bias_ref, mask_ref,
    score_ref, turned_ref, peak_ref,
    part_ref, twin_ref, row_num, row_stat, got_num, got_stat,
    build_num, build_stat, col_num, col_stat, end_num, end_stat,
    load_sem, pair_sem, twin_send, twin_recv, row_send, row_recv, col_send, col_recv,
):
    latent_count, channels = query_ref.shape
    tile_rows, tile_cols = tissue_ref.shape
    tokens = tile_rows * tile_cols
    pairs = heads // 2
    head_dim = channels // heads
    gain = LOG2_E * head_dim ** -0.5
    row_count, half = lax.axis_size("rows"), lax.axis_size("cols") // 2
    own = out_ref.shape[0]
    side_count = latent_count // 2
    per_row = side_count // row_count
    groups = col_num.shape[0]
    per_group = pairs // groups
    row, col = lax.axis_index("rows"), lax.axis_index("cols")
    side, slot = lax.rem(col, 2), lax.div(col, 2)
    twin = (row, slot * 2 + (1 - side))
    row_peers = [(lax.rem(row + step, row_count), col) for step in range(1, row_count)]
    col_peers = [(row, lax.rem(slot + step, half) * 2 + side) for step in range(1, half)]

    load = pltpu.make_async_copy(query_hbm, query_ref, load_sem.at[0])
    late = pltpu.make_async_copy(weight_hbm, weight_ref, load_sem.at[1])

    def fetch(pair, which):
        at = pl.ds(pl.multiple_of(which * channels + pair * LANES, LANES), LANES)
        target = (keys_ref, values_ref)[which]
        return pltpu.make_async_copy(keys_hbm.at[:, at], target.at[pair], pair_sem.at[which, pair])

    load.start()
    for pair in range(pairs):
        fetch(pair, 0).start()
        fetch(pair, 1).start()
    late.start()
    barrier = pltpu.get_barrier_semaphore()
    for peer in [twin] + row_peers + col_peers:
        pl.semaphore_signal(barrier, inc=1, device_id=peer, device_id_type=MESH)

    mask_ref[...] = jnp.zeros_like(mask_ref)
    mask_ref[:, :tile_cols] = jnp.where(tissue_ref[...] > 0, 0.0, LOW)
    spot = lax.broadcasted_iota(jnp.int32, (tile_cols, LANES), 0)
    spot = spot == lax.broadcasted_iota(jnp.int32, (tile_cols, LANES), 1)
    for tile_row in range(tile_rows):
        line = jnp.broadcast_to(mask_ref[tile_row : tile_row + 1, :], (tile_cols, LANES))
        bias_ref[tile_row * tile_cols : (tile_row + 1) * tile_cols, :] = jnp.where(
            spot, line, 0.0
        ).astype(BF16)
    turned_ref[:, head_dim:, :] = jnp.ones((2, CORNER, tokens), BF16)
    build_num[...] = jnp.zeros_like(build_num)
    build_stat[...] = jnp.zeros_like(build_stat)

    lane = lax.broadcasted_iota(jnp.int32, (1, LANES), 1)
    low = lane < head_dim
    query_low = lax.broadcasted_iota(jnp.int32, (latent_count, LANES), 1) < head_dim
    ones = jnp.ones((latent_count, LANES), BF16)
    chunk = tokens // 2
    fresh = jnp.full((8, latent_count), -3e38, F32)

    def asked(pair, which):
        queries = query_ref[:, pl.ds(pl.multiple_of(pair * LANES, LANES), LANES)]
        mine = query_low if which == 0 else jnp.logical_not(query_low)
        return jnp.concatenate([jnp.where(mine, queries, jnp.zeros_like(queries)), ones], 1)

    def score(pair, part, queries, which, peak):
        at = slice(part * chunk, (part + 1) * chunk)
        keys = jnp.concatenate([keys_ref[pair, at, :], bias_ref[at, :]], 1)
        scores = lax.dot_general(
            keys, queries, (((1,), (1,)), ((), ())), preferred_element_type=F32
        )
        score_ref[which, at, :] = scores
        return jnp.maximum(peak, jnp.max(scores.reshape(chunk // 8, 8, latent_count), 0))

    def weigh(part, which, peak, total):
        at = slice(part * chunk, (part + 1) * chunk)
        weights = jnp.exp2((score_ref[which, at, :] - peak) * gain).astype(BF16)
        return total + dot(turned_ref[which, :, at], weights)

    def remote(source, target, send, recv, peer):
        return pltpu.make_async_remote_copy(
            src_ref=source, dst_ref=target, send_sem=send, recv_sem=recv,
            device_id=peer, device_id_type=MESH,
        )

    def to_twin(pair):
        return remote(
            part_ref.at[pair, 1 - side], twin_ref.at[pair],
            twin_send.at[pair], twin_recv.at[pair], twin,
        )

    def to_row(pair, step):
        target = lax.rem(row + step, row_count)
        return [
            remote(
                source.at[pair, target], landing.at[pair, step - 1],
                row_send.at[pair, step - 1, kind], row_recv.at[pair, step - 1, kind],
                row_peers[step - 1],
            )
            for kind, (source, landing) in enumerate(((row_num, got_num), (row_stat, got_stat)))
        ]

    def to_col(group, step):
        target = lax.rem(slot + step, half)
        return [
            remote(
                source.at[group, target], landing.at[group, step - 1],
                col_send.at[group, step - 1, kind], col_recv.at[group, step - 1, kind],
                col_peers[step - 1],
            )
            for kind, (source, landing) in enumerate(((col_num, end_num), (col_stat, end_stat)))
        ]

    first_line = lax.broadcasted_iota(jnp.int32, (8, LANES), 0) == 0
    extent = head_dim + 8

    def with_twin(pair):
        to_twin(pair).wait_recv()
        merged = []
        for which in range(2):
            base = which * extent
            items = []
            for values in (part_ref.at[pair, side], twin_ref.at[pair]):
                stat = values[base + head_dim : base + extent, :]
                items.append((values[base : base + head_dim, :], stat[0:1], stat[1:2]))
            merged.append(merge(items, gain))
        for target in range(row_count):
            tile = target * per_row // LANES
            at = slice(tile * LANES, (tile + 1) * LANES)

            def joined(one, two, target=target, at=at):
                one, two = one[:, at], two[:, at]
                if target * per_row % LANES == 0:
                    return jnp.where(low, one, pltpu.roll(two, per_row, 1))
                return jnp.where(low, pltpu.roll(one, per_row, 1), two)

            number, peak, total = [joined(one, two) for one, two in zip(*merged)]
            row_num[pair, target] = number.astype(BF16)
            row_stat[pair, target] = jnp.where(first_line, peak, total)
        for step in range(1, row_count):
            for copy in to_row(pair, step):
                copy.start()

    def with_rows(pair):
        for step in range(1, row_count):
            for copy in to_row(pair, step):
                copy.wait_recv()
        items = []
        for values, stat in [(row_num[pair, row], row_stat[pair, row])] + [
            (got_num[pair, step], got_stat[pair, step]) for step in range(row_count - 1)
        ]:
            items.append((values.astype(F32), stat[0:1], stat[1:2]))
        number, peak, total = merge(items, gain)
        stat = jnp.where(first_line, peak, total)
        place = lax.rem(pair, per_group) * (2 * own)
        for target in range(half):
            for which in range(2):
                begin = place + which * own
                source = which * head_dim + target * own
                shift = lax.rem(begin - source + LANES, LANES)
                here = jnp.logical_and(lane >= begin, lane < begin + own)
                build_num[target] = jnp.where(
                    here, pltpu.roll(number, shift, 1), build_num[target]
                )
                build_stat[target] = jnp.where(
                    here, pltpu.roll(stat, shift, 1), build_stat[target]
                )

        @pl.when(lax.rem(pair, per_group) == per_group - 1)
        def _():
            group = lax.div(pair, per_group)
            col_num[group] = build_num[...].astype(BF16)
            col_stat[group] = build_stat[...]
            for step in range(1, half):
                for copy in to_col(group, step):
                    copy.start()

    load.wait()
    fetch(0, 0).wait()
    peak = fresh
    queries = asked(0, 0)
    for part in range(2):
        peak = score(0, part, queries, 0, peak)
    peak_ref[...] = peak
    pl.semaphore_wait(barrier, 1 + len(row_peers) + len(col_peers))

    def step(pair, _):
        @pl.when(pair < pairs - 1)
        def _():
            fetch(pair + 1, 0).wait()

        fetch(pair, 1).wait()
        turned = values_ref[pair].T
        for which in range(2):
            turned_ref[which, :head_dim, :] = turned[which * head_dim : (which + 1) * head_dim]
        current = peak_ref[...]
        for which in range(2):
            following = pair if which == 0 else jnp.minimum(pair + 1, pairs - 1)
            queries = asked(following, 1 - which)
            top = jnp.max(current, 0, keepdims=True)
            total = jnp.zeros((head_dim + CORNER, latent_count), F32)
            peak = fresh
            for part in range(2):
                peak = score(following, part, queries, 1 - which, peak)
                total = weigh(part, which, top, total)
            line = lax.broadcasted_iota(jnp.int32, (8, latent_count), 0) == 0
            stat = jnp.where(line, top, total[head_dim : head_dim + 8])
            for half_at in range(2):
                at = slice(half_at * side_count, (half_at + 1) * side_count)
                part_ref[pair, half_at, which * extent : which * extent + head_dim, :] = total[
                    :head_dim, at
                ]
                part_ref[
                    pair, half_at, which * extent + head_dim : (which + 1) * extent, :
                ] = stat[:, at]
            current = peak
        peak_ref[...] = current
        to_twin(pair).start()

        @pl.when(pair >= 1)
        def _():
            with_twin(pair - 1)

        @pl.when(pair >= LAG)
        def _():
            with_rows(pair - LAG)

        return 0

    lax.fori_loop(0, pairs, step, 0)
    for pair in range(pairs - LAG, pairs - 2):
        with_rows(pair)
    with_twin(pairs - 1)
    for pair in range(pairs - 2, pairs):
        with_rows(pair)

    pieces = []
    for group in range(groups):
        items = []
        for step in range(1, half):
            for copy in to_col(group, step):
                copy.wait_recv()
        for values, stat in [(col_num[group, slot], col_stat[group, slot])] + [
            (end_num[group, step], end_stat[group, step]) for step in range(half - 1)
        ]:
            items.append((values.astype(F32), stat[0:1], stat[1:2]))
        number, _, total = merge(items, gain)
        tile = (number / total).T
        for place in range(per_group):
            base = place * 2 * own
            pieces.append(
                jnp.concatenate([tile[base : base + own], tile[base + own : base + 2 * own]], 1)
            )
    attended = jnp.concatenate(pieces, 1)
    mean = jnp.sum(attended * attended, axis=-1, keepdims=True) * (1.0 / channels)
    normed = (attended * lax.rsqrt(mean + 1e-06)).astype(BF16)
    late.wait()
    out_ref[...] = dot(normed, weight_ref[...]).astype(BF16)

    def drain(pair, _):
        to_twin(pair).wait_send()
        for step in range(1, row_count):
            for copy in to_row(pair, step):
                copy.wait_send()
        return 0

    lax.fori_loop(0, pairs, drain, 0)
    for group in range(groups):
        for step in range(1, half):
            for copy in to_col(group, step):
                copy.wait_send()


def attention(tissue, queries, keys, out_weight):
    row_count, col_count = lax.axis_size("rows"), lax.axis_size("cols")
    half = col_count // 2
    latent_count, channels = queries.shape
    tokens = tissue.shape[0] * tissue.shape[1]
    own = latent_count // (row_count * col_count)
    pairs = HEADS // 2
    head_dim = channels // HEADS
    groups = max(1, pairs * 2 * own // LANES)
    side_count = latent_count // 2
    leave = pl.BlockSpec(memory_space=pl.ANY)

    def blocks(*extent):
        return [
            pltpu.VMEM(extent + (head_dim, LANES), BF16), pltpu.VMEM(extent + (8, LANES), F32)
        ]

    def sems(*extent):
        return [pltpu.SemaphoreType.DMA(extent)] * 2

    return pl.pallas_call(
        functools.partial(attend, HEADS),
        out_shape=jax.ShapeDtypeStruct((own, out_weight.shape[1]), BF16),
        in_specs=[pl.BlockSpec(memory_space=pltpu.VMEM)] + [leave] * 3,
        out_specs=pl.BlockSpec(memory_space=pltpu.VMEM),
        scratch_shapes=[
            pltpu.VMEM(queries.shape, BF16),
            pltpu.VMEM((pairs, tokens, LANES), BF16),
            pltpu.VMEM((pairs, tokens, LANES), BF16),
            pltpu.VMEM(out_weight.shape, BF16),
            pltpu.VMEM((tokens, LANES), BF16),
            pltpu.VMEM((tissue.shape[0], LANES), F32),
            pltpu.VMEM((2, tokens, latent_count), F32),
            pltpu.VMEM((2, head_dim + CORNER, tokens), BF16),
            pltpu.VMEM((8, latent_count), F32),
            pltpu.VMEM((pairs, 2, 2 * (head_dim + 8), side_count), F32),
            pltpu.VMEM((pairs, 2 * (head_dim + 8), side_count), F32),
        ]
        + blocks(pairs, row_count)
        + blocks(pairs, row_count - 1)
        + [pltpu.VMEM((half, head_dim, LANES), F32), pltpu.VMEM((half, 8, LANES), F32)]
        + blocks(groups, half)
        + blocks(groups, half - 1)
        + [pltpu.SemaphoreType.DMA((2,)), pltpu.SemaphoreType.DMA((2, pairs))]
        + sems(pairs)
        + sems(pairs, row_count - 1, 2)
        + sems(groups, half - 1, 2),
        compiler_params=pltpu.CompilerParams(
            collective_id=1, has_side_effects=True, vmem_limit_bytes=60 * 1024 * 1024
        ),
        name="attention",
    )(tissue, queries, keys, out_weight)


def shards(pixels, tissue, patch_weight, conv_weight, kv_weight, query_weight, out_weight, latents):
    tile_rows, tile_cols, _ = pixels.shape
    channels = patch_weight.shape[1]
    borders, queries = borders_of(pixels, latents, query_weight)
    features, keys = local_work(borders, pixels, patch_weight, conv_weight, kv_weight)
    latents_out = attention(tissue, queries, keys, out_weight)
    return (features.reshape(tile_rows, tile_cols, channels), latents_out)


def solution(mesh):
    return jax.shard_map(
        shards,
        mesh=mesh,
        in_specs=(P("rows", "cols", None), P("rows", "cols"), P(), P(), P(), P(), P(), P()),
        out_specs=(P("rows", "cols", None), P(("rows", "cols"), None)),
        check_vma=False,
    )
```

time: 76.9 us -> 64.7 us (0.84)
  Pallas kernels: 70.9 us -> 60.4 us
  local copies, waits for them, and re-layouts: 4.31 us -> 3.29 us
    pallas_call x3, Pallas kernels: 70.9 us -> 60.4 us  [the longest x1 28.5 us: attention(): pl.pallas_call(functools.partial(attend, HEADS), out_shape=jax.ShapeDtype...]
    broadcast_in_dim x1 -> x0, local copies, waits for them, and re-layouts: 0.92 us -> none  [shards(): jnp.broadcast_to((tissue.reshape(tokens, 1) > 0).astype(BF16), (tokens, L...]
where the time goes in v1:
time: 64.7 us; the launch traced here: 64.4 us
  Pallas kernels  60.4 us (93%)
  local copies, waits for them, and re-layouts  3.29 us (5%)
  between operations  0.66 us (1%)
    pallas_call x1, Pallas kernels, attention(): pl.pallas_call(functools.partial(attend, HEADS), out_shape=jax.ShapeDtype...  28.5 us
    pallas_call x1, Pallas kernels, local_work(): pl.pallas_call(functools.partial(core, tile_rows, tile_cols), out_shape=(...  19.9 us
    pallas_call x1, Pallas kernels, borders_of(): pl.pallas_call(greet, out_shape=(flat, flat, tall, tall, jax.ShapeDtypeSt...  12 us
    unnamed x1, local copies, waits for them, and re-layouts  1.38 us

profile of v1, /device:TPU:0, one launch (start us, length us, event | category | flops | bytes accessed | tf_op | source)
XLA Modules:
  0.0 64.4 jit_solution(953734563219530404)
XLA Ops:
  0.6 1.3 %fusion = (bf16[32,1,768]{2,1,0:T(2,128)(2,1)S(1)}, bf16[32,1,768]{2,1,0:T(2,128)(2,1)S(1)}) fusion(bf16[32,32,768]{2,1,0:T(8,128)(2,1)} %pixels_ref.1), kind=kLoop, calls=%fused_computation.2 | loop fusion | bytes 196608 | tf_op jit(solution)/shard_map/slice | solution.py:284
  1.9 0.6 copy_bitcast_fusion
  2.5 12.0 %borders.1 = (bf16[32,768]{1,0:T(8,128)(2,1)}, bf16[32,768]{1,0:T(8,128)(2,1)}, bf16[64,768]{1,0:T(8,128)(2,1)}, bf16[64,768]{1,0:T(8,128)(2,1)}, bf16[512,1024]{1,0:T(8,128)(2,1)}) custom-call(bf16[32,32,768]{2,1,0:T(8,128)(2,1)} %pixels_ref.1, bf16[32,768]{1,0:T(8,128)(2,1)} %get-tuple-element.19.first_ref, bf16[32,768]{1,0:T(8,128)(2,1)} %get-tuple-element.18.last_ref, ...), custom_call_target="tpu_custom_call" | custom-call | tf_op jit(solution)/shard_map/borders/pallas_call | solution.py:268
  14.5 19.9 %local_work.1 = (bf16[1024,1024]{1,0:T(8,128)(2,1)}, bf16[1024,2048]{1,0:T(8,128)(2,1)}) custom-call(bf16[32,768]{1,0:T(8,128)(2,1)} %get-tuple-element.9.top_ref, bf16[32,768]{1,0:T(8,128)(2,1)} %get-tuple-element.10.bottom_ref, bf16[64,768]{1,0:T(8,128)(2,1)} %get-tuple-element.11.left_ref, bf16[64,768]{1,0:T(8,128)(2,1)} %get-tuple-element.12.right_ref, ...), custom_call_target="tpu_custom_call" | custom-call | tf_op jit(solution)/shard_map/local_work/pallas_call | solution.py:147
  34.5 28.5 %attention.1 = bf16[16,1024]{1,0:T(8,128)(2,1)} custom-call(s32[32,32]{1,0:T(8,128)} %tissue_ref.1, bf16[512,1024]{1,0:T(8,128)(2,1)} %get-tuple-element.14.query_hbm, bf16[1024,2048]{1,0:T(8,128)(2,1)} %get-tuple-element.15.keys_hbm, bf16[1024,1024]{1,0:T(8,128)(2,1)} %weight_hbm.3), custom_call_target="tpu_custom_call" | custom-call | tf_op jit(solution)/shard_map/attention/pallas_call | solution.py:596
  63.0 1.4 %copy.17 = bf16[16,1024]{1,0:T(8,128)(2,1)} copy(bf16[16,1024]{1,0:T(8,128)(2,1)} %attention.1) | data formatting | bytes 65536

commit v2 on v1

v2 whole, which is shorter than its diff:
```python
import functools

import jax
import jax.numpy as jnp
from jax import lax
from jax.experimental import pallas as pl
from jax.experimental.pallas import tpu as pltpu
from jax.sharding import PartitionSpec as P

HEADS = 16
BLOCK = 256
LANES = 128
PAD = 8
CORNER = 16
LAG = 4
LOG2_E = 1.4426950408889634
F32 = jnp.float32
BF16 = jnp.bfloat16
LOW = -1e30
MESH = pl.DeviceIdType.MESH


def dot(a, b):
    return jnp.dot(a, b, preferred_element_type=F32)


def merge(items, gain):
    top = functools.reduce(jnp.maximum, [peak for _, peak, _ in items])
    number, total = 0.0, 0.0
    for values, peak, whole in items:
        share = jnp.exp2((peak - top) * gain)
        number = number + share * values
        total = total + share * whole
    return number, top, total


def slide(
    heads,
    pixels_hbm, tissue_hbm, patch_hbm, conv_hbm, kv_hbm, ask_hbm, latent_hbm,
    features_hbm, normed_ref,
    pixels_ref, tissue_ref, patch_ref, conv_ref, kv_ref, ask_ref, latent_ref,
    border_ref, side_ref, embedded_ref, wide_ref, taps_ref, summed_ref, features_ref,
    query_ref, keys_ref, turned_ref, bias_ref, mask_ref, score_ref, peak_ref,
    part_ref, twin_ref, row_num, row_stat, got_num, got_stat,
    build_num, build_stat, col_num, col_stat, end_num, end_stat,
    load_sem, halo_send, halo_recv,
    twin_send, twin_recv, row_send, row_recv, col_send, col_recv,
):
    tile_rows, tile_cols, patch_in = pixels_ref.shape
    tokens = tile_rows * tile_cols
    latent_count, channels = query_ref.shape
    pairs = heads // 2
    head_dim = channels // heads
    gain = LOG2_E * head_dim ** -0.5
    group_width = conv_ref.shape[1]
    row_count, col_count = lax.axis_size("rows"), lax.axis_size("cols")
    half = col_count // 2
    own = normed_ref.shape[0]
    side_count = latent_count // 2
    per_row = side_count // row_count
    groups = col_num.shape[0]
    per_group = pairs // groups
    row, col = lax.axis_index("rows"), lax.axis_index("cols")
    side, slot = lax.rem(col, 2), lax.div(col, 2)
    twin = (row, slot * 2 + (1 - side))
    row_peers = [(lax.rem(row + step, row_count), col) for step in range(1, row_count)]
    col_peers = [(row, lax.rem(slot + step, half) * 2 + side) for step in range(1, half)]

    loads = [
        pltpu.make_async_copy(source, target, load_sem.at[number])
        for number, (source, target) in enumerate(
            (
                (pixels_hbm, pixels_ref), (patch_hbm, patch_ref),
                (latent_hbm.at[:, :, 0], latent_ref.at[0]),
                (latent_hbm.at[:, :, 1], latent_ref.at[1]),
                (ask_hbm, ask_ref), (conv_hbm, conv_ref), (tissue_hbm, tissue_ref),
                (kv_hbm, kv_ref),
            )
        )
    ]
    for load in loads:
        load.start()

    low_cols, high_cols = slice(0, CORNER), slice(tile_cols - CORNER, tile_cols)
    top, bottom = 0, tile_cols
    left = 2 * tile_cols
    right = left + tile_rows + 2 * CORNER
    end = tile_rows - 1

    def landing(start, extent):
        return border_ref.at[start : start + extent]

    moves = (
        (1, 0, pixels_hbm.at[end], landing(top, tile_cols)),
        (-1, 0, pixels_hbm.at[0], landing(bottom, tile_cols)),
        (1, 1, pixels_hbm.at[end, high_cols], landing(left + tile_rows, CORNER)),
        (1, -1, pixels_hbm.at[end, low_cols], landing(right + tile_rows, CORNER)),
        (-1, 1, pixels_hbm.at[0, high_cols], landing(left + tile_rows + CORNER, CORNER)),
        (-1, -1, pixels_hbm.at[0, low_cols], landing(right + tile_rows + CORNER, CORNER)),
        (0, 1, side_ref.at[1], landing(left, tile_rows)),
        (0, -1, side_ref.at[0], landing(right, tile_rows)),
    )

    def inside(down, across):
        ok = None
        for at, step, count in ((row, down, row_count), (col, across, col_count)):
            if step:
                here = at + step < count if step > 0 else at + step >= 0
                ok = here if ok is None else jnp.logical_and(ok, here)
        return ok

    def shift(number):
        down, across, source, target = moves[number]
        return pltpu.make_async_remote_copy(
            src_ref=source, dst_ref=target,
            send_sem=halo_send.at[number], recv_sem=halo_recv.at[number],
            device_id=(row + down, col + across), device_id_type=MESH,
        )

    barrier = pltpu.get_barrier_semaphore()
    for down, across, _, _ in moves:
        @pl.when(inside(down, across))
        def _(down=down, across=across):
            pl.semaphore_signal(
                barrier, inc=1, device_id=(row + down, col + across), device_id_type=MESH
            )
    for peer in [twin] + row_peers + col_peers:
        pl.semaphore_signal(barrier, inc=1, device_id=peer, device_id_type=MESH)
    tall = 1 + (row > 0).astype(jnp.int32) + (row < row_count - 1).astype(jnp.int32)
    broad = 1 + (col > 0).astype(jnp.int32) + (col < col_count - 1).astype(jnp.int32)
    turned_ref[:, :, head_dim:, :] = jnp.ones((pairs, 2, CORNER, tokens), BF16)
    build_num[...] = jnp.zeros_like(build_num)
    build_stat[...] = jnp.zeros_like(build_stat)
    pl.semaphore_wait(barrier, tall * broad - 1 + 1 + len(row_peers) + len(col_peers))
    for number in range(6):
        @pl.when(inside(*moves[number][:2]))
        def _(number=number):
            shift(number).start()
    loads[0].wait()
    side_ref[0] = pixels_ref[:, 0, :]
    side_ref[1] = pixels_ref[:, tile_cols - 1, :]
    for number in range(6, 8):
        @pl.when(inside(*moves[number][:2]))
        def _(number=number):
            shift(number).start()
    loads[1].wait()

    def embed(step, _):
        at = pl.ds(pl.multiple_of(step * BLOCK, BLOCK), BLOCK)
        pixels = pixels_ref[...].reshape(tokens, patch_in)
        embedded_ref[:, at] = dot(pixels, patch_ref[:, at])
        return 0

    lax.fori_loop(0, channels // BLOCK, embed, 0)
    for load in loads[2:5]:
        load.wait()

    def ask(step, _):
        at = pl.ds(pl.multiple_of(step * BLOCK, BLOCK), BLOCK)
        latents = latent_ref[...].reshape(latent_count, ask_ref.shape[0])
        query_ref[:, at] = dot(latents, ask_ref[:, at]).astype(BF16)
        return 0

    lax.fori_loop(0, channels // BLOCK, ask, 0)
    for load in loads[5:7]:
        load.wait()
    mask_ref[...] = jnp.zeros_like(mask_ref)
    mask_ref[:, :tile_cols] = jnp.where(tissue_ref[...] > 0, 0.0, LOW)
    spot = lax.broadcasted_iota(jnp.int32, (tile_cols, LANES), 0)
    spot = spot == lax.broadcasted_iota(jnp.int32, (tile_cols, LANES), 1)
    for tile_row in range(tile_rows):
        line = jnp.broadcast_to(mask_ref[tile_row : tile_row + 1, :], (tile_cols, LANES))
        bias_ref[tile_row * tile_cols : (tile_row + 1) * tile_cols, :] = jnp.where(
            spot, line, 0.0
        ).astype(BF16)
    for number, (down, across, _, target) in enumerate(moves):
        @pl.when(inside(-down, -across))
        def _(number=number):
            shift(number).wait_recv()

        @pl.when(jnp.logical_not(inside(-down, -across)))
        def _(target=target):
            target[...] = jnp.zeros(target.shape, BF16)

    rows_ext = tile_rows + 2
    col_ext = tile_cols + PAD
    same = (
        lax.broadcasted_iota(jnp.int32, (BLOCK, BLOCK), 0) // group_width
        == lax.broadcasted_iota(jnp.int32, (BLOCK, BLOCK), 1) // group_width
    )
    side_slot = lax.broadcasted_iota(jnp.int32, (rows_ext, PAD, BLOCK), 1)
    thin = (1, PAD, BLOCK)

    def border(values, upper, lower):
        return (
            jnp.broadcast_to(values[upper : upper + 1][:, None, :], thin),
            jnp.broadcast_to(values[:tile_rows][:, None, :], (tile_rows, PAD, BLOCK)),
            jnp.broadcast_to(values[lower : lower + 1][:, None, :], thin),
        )

    for block in range(channels // BLOCK):
        lanes = slice(block * BLOCK, (block + 1) * BLOCK)
        edges = dot(border_ref[...], patch_ref[:, lanes])
        inner = jnp.concatenate(
            [edges[top:bottom], embedded_ref[:, lanes], edges[bottom:left]], 0
        )
        upper, middle, lower = border(
            edges[left:right], tile_rows + CORNER - 1, tile_rows + 2 * CORNER - 1
        )
        from_left = jnp.concatenate([middle, lower, upper], 0)
        upper, middle, lower = border(edges[right:], tile_rows, tile_rows + CORNER)
        from_right = jnp.concatenate([upper, middle, lower], 0)
        flank = jnp.where(side_slot == PAD - 1, from_left, from_right)
        full = jnp.concatenate(
            [inner.reshape(rows_ext, tile_cols, BLOCK), flank], 1
        ).reshape(rows_ext * col_ext, BLOCK)
        for col_shift, amount in ((0, 1), (2, rows_ext * col_ext - 1)):
            moved = pltpu.roll(full, amount, 0).reshape(rows_ext, col_ext, BLOCK)
            moved = moved[:, :tile_cols].reshape(rows_ext * tile_cols, BLOCK)
            wide_ref[:, col_shift * BLOCK : (col_shift + 1) * BLOCK] = moved.astype(BF16)
        wide_ref[:, BLOCK : 2 * BLOCK] = inner.astype(BF16)
        for tap in range(9):
            small = conv_ref[tap, :, lanes]
            tiled = jnp.concatenate([small] * (BLOCK // group_width), 0)
            row_shift, col_shift = tap // 3, tap % 3
            taps_ref[row_shift, col_shift * BLOCK : (col_shift + 1) * BLOCK, :] = jnp.where(
                same, tiled, jnp.zeros_like(tiled)
            )
        total = wide_ref[tile_cols : tile_cols + tokens, BLOCK : 2 * BLOCK].astype(F32)
        for row_shift in range(3):
            first = row_shift * tile_cols
            total = total + dot(wide_ref[first : first + tokens, :], taps_ref[row_shift])
        summed_ref[:, lanes] = total

    piece = 128
    inverse = 1.0 / channels

    def normalise(step, _):
        at = pl.ds(pl.multiple_of(step * piece, piece), piece)
        values = summed_ref[at, :]
        centred = values - jnp.sum(values, axis=-1, keepdims=True) * inverse
        variance = jnp.sum(centred * centred, axis=-1, keepdims=True) * inverse
        features_ref[at, :] = (centred * lax.rsqrt(variance + 1e-05)).astype(BF16)
        return 0

    lax.fori_loop(0, tokens // piece, normalise, 0)
    store = pltpu.make_async_copy(features_ref, features_hbm, load_sem.at[len(loads)])
    store.start()
    loads[7].wait()

    def project(step, _):
        for base in (0, channels):
            at = pl.ds(pl.multiple_of(base + step * BLOCK, BLOCK), BLOCK)
            found = dot(features_ref[...], kv_ref[:, at]).astype(BF16)
            for inner in range(BLOCK // LANES):
                pair = step * (BLOCK // LANES) + inner
                mine = found[:, inner * LANES : (inner + 1) * LANES]
                if base == 0:
                    keys_ref[pair] = mine
                else:
                    mine = mine.T
                    for which in range(2):
                        turned_ref[pair, which, :head_dim, :] = mine[
                            which * head_dim : (which + 1) * head_dim
                        ]
        return 0

    lax.fori_loop(0, channels // BLOCK, project, 0)

    lane = lax.broadcasted_iota(jnp.int32, (1, LANES), 1)
    low = lane < head_dim
    query_low = lax.broadcasted_iota(jnp.int32, (latent_count, LANES), 1) < head_dim
    ones = jnp.ones((latent_count, LANES), BF16)
    chunk = tokens // 2
    fresh = jnp.full((8, latent_count), -3e38, F32)

    def asked(pair, which):
        queries = query_ref[:, pl.ds(pl.multiple_of(pair * LANES, LANES), LANES)]
        mine = query_low if which == 0 else jnp.logical_not(query_low)
        return jnp.concatenate([jnp.where(mine, queries, jnp.zeros_like(queries)), ones], 1)

    def score(pair, part, queries, which, peak):
        at = slice(part * chunk, (part + 1) * chunk)
        keys = jnp.concatenate([keys_ref[pair, at, :], bias_ref[at, :]], 1)
        scores = lax.dot_general(
            keys, queries, (((1,), (1,)), ((), ())), preferred_element_type=F32
        )
        score_ref[which, at, :] = scores
        return jnp.maximum(peak, jnp.max(scores.reshape(chunk // 8, 8, latent_count), 0))

    def weigh(pair, part, which, peak, total):
        at = slice(part * chunk, (part + 1) * chunk)
        weights = jnp.exp2((score_ref[which, at, :] - peak) * gain).astype(BF16)
        return total + dot(turned_ref[pair, which, :, at], weights)

    def remote(source, target, send, recv, peer):
        return pltpu.make_async_remote_copy(
            src_ref=source, dst_ref=target, send_sem=send, recv_sem=recv,
            device_id=peer, device_id_type=MESH,
        )

    def to_twin(pair):
        return remote(
            part_ref.at[pair, 1 - side], twin_ref.at[pair],
            twin_send.at[pair], twin_recv.at[pair], twin,
        )

    def to_row(pair, step):
        target = lax.rem(row + step, row_count)
        return [
            remote(
                source.at[pair, target], landing.at[pair, step - 1],
                row_send.at[pair, step - 1, kind], row_recv.at[pair, step - 1, kind],
                row_peers[step - 1],
            )
            for kind, (source, landing) in enumerate(((row_num, got_num), (row_stat, got_stat)))
        ]

    def to_col(group, step):
        target = lax.rem(slot + step, half)
        return [
            remote(
                source.at[group, target], landing.at[group, step - 1],
                col_send.at[group, step - 1, kind], col_recv.at[group, step - 1, kind],
                col_peers[step - 1],
            )
            for kind, (source, landing) in enumerate(((col_num, end_num), (col_stat, end_stat)))
        ]

    first_line = lax.broadcasted_iota(jnp.int32, (8, LANES), 0) == 0
    extent = head_dim + 8

    def with_twin(pair):
        to_twin(pair).wait_recv()
        merged = []
        for which in range(2):
            base = which * extent
            items = []
            for values in (part_ref.at[pair, side], twin_ref.at[pair]):
                stat = values[base + head_dim : base + extent, :]
                items.append((values[base : base + head_dim, :], stat[0:1], stat[1:2]))
            merged.append(merge(items, gain))
        for target in range(row_count):
            tile = target * per_row // LANES
            at = slice(tile * LANES, (tile + 1) * LANES)

            def joined(one, two, target=target, at=at):
                one, two = one[:, at], two[:, at]
                if target * per_row % LANES == 0:
                    return jnp.where(low, one, pltpu.roll(two, per_row, 1))
                return jnp.where(low, pltpu.roll(one, per_row, 1), two)

            number, peak, total = [joined(one, two) for one, two in zip(*merged)]
            row_num[pair, target] = number.astype(BF16)
            row_stat[pair, target] = jnp.where(first_line, peak, total)
        for step in range(1, row_count):
            for copy in to_row(pair, step):
                copy.start()

    def with_rows(pair):
        for step in range(1, row_count):
            for copy in to_row(pair, step):
                copy.wait_recv()
        items = []
        for values, stat in [(row_num[pair, row], row_stat[pair, row])] + [
            (got_num[pair, step], got_stat[pair, step]) for step in range(row_count - 1)
        ]:
            items.append((values.astype(F32), stat[0:1], stat[1:2]))
        number, peak, total = merge(items, gain)
        stat = jnp.where(first_line, peak, total)
        place = lax.rem(pair, per_group) * (2 * own)
        for target in range(half):
            for which in range(2):
                begin = place + which * own
                source = which * head_dim + target * own
                shift = lax.rem(begin - source + LANES, LANES)
                here = jnp.logical_and(lane >= begin, lane < begin + own)
                build_num[target] = jnp.where(
                    here, pltpu.roll(number, shift, 1), build_num[target]
                )
                build_stat[target] = jnp.where(
                    here, pltpu.roll(stat, shift, 1), build_stat[target]
                )

        @pl.when(lax.rem(pair, per_group) == per_group - 1)
        def _():
            group = lax.div(pair, per_group)
            col_num[group] = build_num[...].astype(BF16)
            col_stat[group] = build_stat[...]
            for step in range(1, half):
                for copy in to_col(group, step):
                    copy.start()

    peak = fresh
    queries = asked(0, 0)
    for part in range(2):
        peak = score(0, part, queries, 0, peak)
    peak_ref[...] = peak

    def step(pair, _):
        current = peak_ref[...]
        for which in range(2):
            following = pair if which == 0 else jnp.minimum(pair + 1, pairs - 1)
            queries = asked(following, 1 - which)
            top = jnp.max(current, 0, keepdims=True)
            total = jnp.zeros((head_dim + CORNER, latent_count), F32)
            peak = fresh
            for part in range(2):
                peak = score(following, part, queries, 1 - which, peak)
                total = weigh(pair, part, which, top, total)
            line = lax.broadcasted_iota(jnp.int32, (8, latent_count), 0) == 0
            stat = jnp.where(line, top, total[head_dim : head_dim + 8])
            for half_at in range(2):
                at = slice(half_at * side_count, (half_at + 1) * side_count)
                part_ref[pair, half_at, which * extent : which * extent + head_dim, :] = total[
                    :head_dim, at
                ]
                part_ref[
                    pair, half_at, which * extent + head_dim : (which + 1) * extent, :
                ] = stat[:, at]
            current = peak
        peak_ref[...] = current
        to_twin(pair).start()

        @pl.when(pair >= 1)
        def _():
            with_twin(pair - 1)

        @pl.when(pair >= LAG)
        def _():
            with_rows(pair - LAG)

        return 0

    lax.fori_loop(0, pairs, step, 0)
    for pair in range(pairs - LAG, pairs - 2):
        with_rows(pair)
    with_twin(pairs - 1)
    for pair in range(pairs - 2, pairs):
        with_rows(pair)

    pieces = []
    for group in range(groups):
        items = []
        for step in range(1, half):
            for copy in to_col(group, step):
                copy.wait_recv()
        for values, stat in [(col_num[group, slot], col_stat[group, slot])] + [
            (end_num[group, step], end_stat[group, step]) for step in range(half - 1)
        ]:
            items.append((values.astype(F32), stat[0:1], stat[1:2]))
        number, _, total = merge(items, gain)
        tile = (number / total).T
        for place in range(per_group):
            base = place * 2 * own
            pieces.append(
                jnp.concatenate([tile[base : base + own], tile[base + own : base + 2 * own]], 1)
            )
    attended = jnp.concatenate(pieces, 1)
    mean = jnp.sum(attended * attended, axis=-1, keepdims=True) * (1.0 / channels)
    normed = (attended * lax.rsqrt(mean + 1e-06)).astype(BF16)
    normed_ref[...] = normed

    def drain(pair, _):
        to_twin(pair).wait_send()
        for step in range(1, row_count):
            for copy in to_row(pair, step):
                copy.wait_send()
        return 0

    lax.fori_loop(0, pairs, drain, 0)
    for group in range(groups):
        for step in range(1, half):
            for copy in to_col(group, step):
                copy.wait_send()
    store.wait()
    for number, (down, across, _, _) in enumerate(moves):
        @pl.when(inside(down, across))
        def _(number=number):
            shift(number).wait_send()


def embed_attend(pixels, tissue, patch_weight, conv_weight, kv_weight, query_weight, latents):
    tile_rows, tile_cols, patch_in = pixels.shape
    tokens = tile_rows * tile_cols
    row_count, col_count = lax.axis_size("rows"), lax.axis_size("cols")
    half = col_count // 2
    latent_count = latents.shape[0]
    channels = query_weight.shape[1]
    own = latent_count // (row_count * col_count)
    pairs = HEADS // 2
    head_dim = channels // HEADS
    groups = max(1, pairs * 2 * own // LANES)
    side_count = latent_count // 2
    leave = pl.BlockSpec(memory_space=pl.ANY)
    latents = latents.reshape(row_count, half, 2, own, latents.shape[1])
    borders = 2 * tile_cols + 2 * (tile_rows + 2 * CORNER)

    def like(array):
        return pltpu.VMEM(array.shape, array.dtype)

    def blocks(*extent):
        return [
            pltpu.VMEM(extent + (head_dim, LANES), BF16), pltpu.VMEM(extent + (8, LANES), F32)
        ]

    def sems(*extent):
        return [pltpu.SemaphoreType.DMA(extent)] * 2

    return pl.pallas_call(
        functools.partial(slide, HEADS),
        out_shape=(
            jax.ShapeDtypeStruct((tokens, channels), BF16),
            jax.ShapeDtypeStruct((own, channels), BF16),
        ),
        in_specs=[leave] * 7,
        out_specs=(leave, pl.BlockSpec(memory_space=pltpu.VMEM)),
        scratch_shapes=[
            like(array)
            for array in (pixels, tissue, patch_weight, conv_weight, kv_weight, query_weight)
        ]
        + [
            pltpu.VMEM((2, row_count, half, own, latents.shape[-1]), BF16),
            pltpu.VMEM((borders, patch_in), BF16),
            pltpu.VMEM((2, tile_rows, patch_in), BF16),
            pltpu.VMEM((tokens, channels), F32),
            pltpu.VMEM(((tile_rows + 2) * tile_cols, 3 * BLOCK), BF16),
            pltpu.VMEM((3, 3 * BLOCK, BLOCK), BF16),
            pltpu.VMEM((tokens, channels), F32),
            pltpu.VMEM((tokens, channels), BF16),
            pltpu.VMEM((latent_count, channels), BF16),
            pltpu.VMEM((pairs, tokens, LANES), BF16),
            pltpu.VMEM((pairs, 2, head_dim + CORNER, tokens), BF16),
            pltpu.VMEM((tokens, LANES), BF16),
            pltpu.VMEM((tile_rows, LANES), F32),
            pltpu.VMEM((2, tokens, latent_count), F32),
            pltpu.VMEM((8, latent_count), F32),
            pltpu.VMEM((pairs, 2, 2 * (head_dim + 8), side_count), F32),
            pltpu.VMEM((pairs, 2 * (head_dim + 8), side_count), F32),
        ]
        + blocks(pairs, row_count)
        + blocks(pairs, row_count - 1)
        + [pltpu.VMEM((half, head_dim, LANES), F32), pltpu.VMEM((half, 8, LANES), F32)]
        + blocks(groups, half)
        + blocks(groups, half - 1)
        + [pltpu.SemaphoreType.DMA((9,))]
        + sems(8)
        + sems(pairs)
        + sems(pairs, row_count - 1, 2)
        + sems(groups, half - 1, 2),
        compiler_params=pltpu.CompilerParams(
            collective_id=1, has_side_effects=True, vmem_limit_bytes=60 * 1024 * 1024
        ),
        name="slide",
    )(pixels, tissue, patch_weight, conv_weight, kv_weight, query_weight, latents)


def finish(
    features_hbm, normed_ref, weight_hbm,
    copied_hbm, out_ref,
    features_ref, weight_ref, in_sem, out_sem, load_sem,
):
    parts = in_sem.shape[0]
    extent = features_ref.shape[0] // parts
    load = pltpu.make_async_copy(weight_hbm, weight_ref, load_sem)

    def fetch(part):
        at = pl.ds(part * extent, extent)
        return pltpu.make_async_copy(features_hbm.at[at], features_ref.at[at], in_sem.at[part])

    def store(part):
        at = pl.ds(part * extent, extent)
        return pltpu.make_async_copy(features_ref.at[at], copied_hbm.at[at], out_sem.at[part])

    for part in range(parts):
        fetch(part).start()
    load.start()
    for part in range(parts):
        fetch(part).wait()
        store(part).start()
    load.wait()
    out_ref[...] = dot(normed_ref[...], weight_ref[...]).astype(BF16)
    for part in range(parts):
        store(part).wait()


def place(features, normed, out_weight):
    leave = pl.BlockSpec(memory_space=pl.ANY)
    vmem = pl.BlockSpec(memory_space=pltpu.VMEM)
    parts = 4
    return pl.pallas_call(
        finish,
        out_shape=(
            jax.ShapeDtypeStruct(features.shape, BF16),
            jax.ShapeDtypeStruct((normed.shape[0], out_weight.shape[1]), BF16),
        ),
        in_specs=[leave, vmem, leave],
        out_specs=(leave, vmem),
        scratch_shapes=[
            pltpu.VMEM(features.shape, BF16),
            pltpu.VMEM(out_weight.shape, BF16),
            pltpu.SemaphoreType.DMA((parts,)),
            pltpu.SemaphoreType.DMA((parts,)),
            pltpu.SemaphoreType.DMA,
        ],
        compiler_params=pltpu.CompilerParams(vmem_limit_bytes=32 * 1024 * 1024),
        name="place",
    )(features, normed, out_weight)


def shards(pixels, tissue, patch_weight, conv_weight, kv_weight, query_weight, out_weight, latents):
    tile_rows, tile_cols, _ = pixels.shape
    features, normed = embed_attend(
        pixels, tissue, patch_weight, conv_weight, kv_weight, query_weight, latents
    )
    features, latents_out = place(features, normed, out_weight)
    return (features.reshape(tile_rows, tile_cols, features.shape[1]), latents_out)


def solution(mesh):
    return jax.shard_map(
        shards,
        mesh=mesh,
        in_specs=(P("rows", "cols", None), P("rows", "cols"), P(), P(), P(), P(), P(), P()),
        out_specs=(P("rows", "cols", None), P(("rows", "cols"), None)),
        check_vma=False,
    )
```

time: 64.7 us -> 53.8 us (0.83)
  Pallas kernels: 60.4 us -> 50.5 us
  local copies, waits for them, and re-layouts: 3.29 us -> 2.35 us
    pallas_call x3 -> x2, Pallas kernels: 60.4 us -> 50.5 us  [the longest x1 48.3 us: embed_attend(): pl.pallas_call(functools.partial(slide, HEADS), out_shape=(jax.ShapeDtype...]
    slice x1 -> x0, local copies, waits for them, and re-layouts: 1.28 us -> none  [borders_of(): pixels[:, -1]]
    unnamed x1 -> x6, local copies, waits for them, and re-layouts: 1.38 us -> 2.35 us
where the time goes in v2:
time: 53.8 us; the launch traced here: 53.6 us
  Pallas kernels  50.5 us (94%)
  local copies, waits for them, and re-layouts  2.35 us (4%)
  between operations  0.67 us (1%)
    pallas_call x1, Pallas kernels, embed_attend(): pl.pallas_call(functools.partial(slide, HEADS), out_shape=(jax.ShapeDtype...  48.3 us
    unnamed x6, local copies, waits for them, and re-layouts  2.35 us
    pallas_call x1, Pallas kernels, place(): pl.pallas_call(finish, out_shape=(jax.ShapeDtypeStruct(features.shape, BF...  2.28 us

profile of v2, /device:TPU:0, one launch (start us, length us, event | category | flops | bytes accessed | tf_op | source)
XLA Modules:
  0.0 53.6 jit_solution(3828313497715988183)
XLA Ops:
  0.6 0.0 copy-start
  0.6 48.3 %slide.1 = (bf16[1024,1024]{1,0:T(8,128)(2,1)}, bf16[16,1024]{1,0:T(8,128)(2,1)}) custom-call(bf16[32,32,768]{2,1,0:T(8,128)(2,1)} %pixels_hbm.1, s32[32,32]{1,0:T(8,128)} %tissue_hbm.1, bf16[768,1024]{1,0:T(8,128)(2,1)} %patch_hbm.1, bf16[9,32,1024]{2,1,0:T(8,128)(2,1)} %conv_hbm.1, bf16[1024,2048]{1,0:T(8,128)(2,1)} %kv_hbm.1, bf16[1024,1024]{1,0:T(8,128)(2,1)} %ask_hbm.1, ...), custom_call_target="tpu_custom_call" | custom-call | tf_op jit(solution)/shard_map/slide/pallas_call | solution.py:510
  48.9 0.0 copy-done
  48.9 0.0 copy-start.1
  48.9 1.6 %copy-done.1 = bf16[1024,1024]{1,0:T(8,128)(2,1)S(1)} copy-done((bf16[1024,1024]{1,0:T(8,128)(2,1)S(1)}, bf16[1024,1024]{1,0:T(8,128)(2,1)}, u32[]{:S(2)}) %copy-start.1) | copy-done | bytes 2097176
  50.5 0.0 copy-start.2
  50.5 0.8 %copy-done.2 = bf16[16,1024]{1,0:T(8,128)(2,1)S(1)} copy-done((bf16[16,1024]{1,0:T(8,128)(2,1)S(1)}, bf16[16,1024]{1,0:T(8,128)(2,1)}, u32[]{:S(2)}) %copy-start.2) | copy-done | bytes 32792
  51.3 2.3 %place.1 = (bf16[1024,1024]{1,0:T(8,128)(2,1)}, bf16[16,1024]{1,0:T(8,128)(2,1)}) custom-call(bf16[1024,1024]{1,0:T(8,128)(2,1)S(1)} %copy-done.1, bf16[16,1024]{1,0:T(8,128)(2,1)S(1)} %copy-done.2, bf16[1024,1024]{1,0:T(8,128)(2,1)S(1)} %copy-done), custom_call_target="tpu_custom_call" | custom-call | tf_op jit(solution)/shard_map/place/pallas_call | solution.py:591
Async XLA Ops:
  0.6 48.3 %copy-start = (bf16[1024,1024]{1,0:T(8,128)(2,1)S(1)}, bf16[1024,1024]{1,0:T(8,128)(2,1)}, u32[]{:S(2)}) copy-start(bf16[1024,1024]{1,0:T(8,128)(2,1)} %weight_hbm.1) | copy-start | bytes 6291460
  48.9 1.6 %copy-start.1 = (bf16[1024,1024]{1,0:T(8,128)(2,1)S(1)}, bf16[1024,1024]{1,0:T(8,128)(2,1)}, u32[]{:S(2)}) copy-start(bf16[1024,1024]{1,0:T(8,128)(2,1)} %get-tuple-element.6.features_hbm) | copy-start | bytes 6291460
  50.5 0.8 %copy-start.2 = (bf16[16,1024]{1,0:T(8,128)(2,1)S(1)}, bf16[16,1024]{1,0:T(8,128)(2,1)}, u32[]{:S(2)}) copy-start(bf16[16,1024]{1,0:T(8,128)(2,1)} %get-tuple-element.7.normed_ref) | copy-start | bytes 98308

commit v3 on v2

--- a/solution.py
+++ b/solution.py
@@ -37,13 +37,13 @@
 def slide(
     heads,
     pixels_hbm, tissue_hbm, patch_hbm, conv_hbm, kv_hbm, ask_hbm, latent_hbm,
-    features_hbm, normed_ref,
+    features_ref, normed_ref,
     pixels_ref, tissue_ref, patch_ref, conv_ref, kv_ref, ask_ref, latent_ref,
-    border_ref, side_ref, embedded_ref, wide_ref, taps_ref, summed_ref, features_ref,
+    border_ref, side_ref, embedded_ref, wide_ref, taps_ref, summed_ref,
     query_ref, keys_ref, turned_ref, bias_ref, mask_ref, score_ref, peak_ref,
     part_ref, twin_ref, row_num, row_stat, got_num, got_stat,
     build_num, build_stat, col_num, col_stat, end_num, end_stat,
-    load_sem, halo_send, halo_recv,
+    load_sem, patch_sem, ask_send, ask_recv, halo_send, halo_recv,
     twin_send, twin_recv, row_send, row_recv, col_send, col_recv,
 ):
     tile_rows, tile_cols, patch_in = pixels_ref.shape
@@ -66,20 +66,29 @@
     row_peers = [(lax.rem(row + step, row_count), col) for step in range(1, row_count)]
     col_peers = [(row, lax.rem(slot + step, half) * 2 + side) for step in range(1, half)]
 
-    loads = [
-        pltpu.make_async_copy(source, target, load_sem.at[number])
-        for number, (source, target) in enumerate(
+    fetches = {
+        name: pltpu.make_async_copy(source, target, load_sem.at[number])
+        for number, (name, source, target) in enumerate(
             (
-                (pixels_hbm, pixels_ref), (patch_hbm, patch_ref),
-                (latent_hbm.at[:, :, 0], latent_ref.at[0]),
-                (latent_hbm.at[:, :, 1], latent_ref.at[1]),
-                (ask_hbm, ask_ref), (conv_hbm, conv_ref), (tissue_hbm, tissue_ref),
-                (kv_hbm, kv_ref),
+                ("pixels", pixels_hbm, pixels_ref),
+                ("low", latent_hbm.at[:, :, 0], latent_ref.at[0]),
+                ("high", latent_hbm.at[:, :, 1], latent_ref.at[1]),
+                ("ask", ask_hbm, ask_ref), ("conv", conv_hbm, conv_ref),
+                ("tissue", tissue_hbm, tissue_ref), ("kv", kv_hbm, kv_ref),
             )
         )
-    ]
-    for load in loads:
-        load.start()
+    }
+    blocks = channels // BLOCK
+
+    def patch_load(step):
+        at = pl.ds(pl.multiple_of(step * BLOCK, BLOCK), BLOCK)
+        return pltpu.make_async_copy(
+            patch_hbm.at[:, at], patch_ref.at[:, at], patch_sem.at[step]
+        )
+
+    fetches["pixels"].start()
+    for block in range(blocks):
+        patch_load(block).start()
 
     low_cols, high_cols = slice(0, CORNER), slice(tile_cols - CORNER, tile_cols)
     top, bottom = 0, tile_cols
@@ -115,6 +124,12 @@
             src_ref=source, dst_ref=target,
             send_sem=halo_send.at[number], recv_sem=halo_recv.at[number],
             device_id=(row + down, col + across), device_id_type=MESH,
+        )
+
+    def remote(source, target, send, recv, peer):
+        return pltpu.make_async_remote_copy(
+            src_ref=source, dst_ref=target, send_sem=send, recv_sem=recv,
+            device_id=peer, device_id_type=MESH,
         )
 
     barrier = pltpu.get_barrier_semaphore()
@@ -128,7 +143,7 @@
         pl.semaphore_signal(barrier, inc=1, device_id=peer, device_id_type=MESH)
     tall = 1 + (row > 0).astype(jnp.int32) + (row < row_count - 1).astype(jnp.int32)
     broad = 1 + (col > 0).astype(jnp.int32) + (col < col_count - 1).astype(jnp.int32)
-    turned_ref[:, :, head_dim:, :] = jnp.ones((pairs, 2, CORNER, tokens), BF16)
+    turned_ref[:, head_dim:, :] = jnp.ones((2, CORNER, tokens), BF16)
     build_num[...] = jnp.zeros_like(build_num)
     build_stat[...] = jnp.zeros_like(build_stat)
     pl.semaphore_wait(barrier, tall * broad - 1 + 1 + len(row_peers) + len(col_peers))
@@ -136,34 +151,46 @@
         @pl.when(inside(*moves[number][:2]))
         def _(number=number):
             shift(number).start()
-    loads[0].wait()
+    fetches["pixels"].wait()
     side_ref[0] = pixels_ref[:, 0, :]
     side_ref[1] = pixels_ref[:, tile_cols - 1, :]
     for number in range(6, 8):
         @pl.when(inside(*moves[number][:2]))
         def _(number=number):
             shift(number).start()
-    loads[1].wait()
+    for name in ("low", "high", "ask", "conv", "tissue", "kv"):
+        fetches[name].start()
 
     def embed(step, _):
         at = pl.ds(pl.multiple_of(step * BLOCK, BLOCK), BLOCK)
+        patch_load(step).wait()
         pixels = pixels_ref[...].reshape(tokens, patch_in)
         embedded_ref[:, at] = dot(pixels, patch_ref[:, at])
         return 0
 
-    lax.fori_loop(0, channels // BLOCK, embed, 0)
-    for load in loads[2:5]:
-        load.wait()
+    lax.fori_loop(0, blocks, embed, 0)
+    for name in ("low", "high", "ask"):
+        fetches[name].wait()
+    shared = blocks - blocks // 4
+    mine_from = jnp.where(side == 0, 0, shared)
+    mine_to = jnp.where(side == 0, shared, blocks)
+
+    def share(step):
+        at = pl.ds(pl.multiple_of(step * BLOCK, BLOCK), BLOCK)
+        return remote(
+            query_ref.at[:, at], query_ref.at[:, at], ask_send.at[step], ask_recv.at[step], twin
+        )
 
     def ask(step, _):
         at = pl.ds(pl.multiple_of(step * BLOCK, BLOCK), BLOCK)
         latents = latent_ref[...].reshape(latent_count, ask_ref.shape[0])
         query_ref[:, at] = dot(latents, ask_ref[:, at]).astype(BF16)
-        return 0
-
-    lax.fori_loop(0, channels // BLOCK, ask, 0)
-    for load in loads[5:7]:
-        load.wait()
+        share(step).start()
+        return 0
+
+    lax.fori_loop(mine_from, mine_to, ask, 0)
+    for name in ("conv", "tissue"):
+        fetches[name].wait()
     mask_ref[...] = jnp.zeros_like(mask_ref)
     mask_ref[:, :tile_cols] = jnp.where(tissue_ref[...] > 0, 0.0, LOW)
     spot = lax.broadcasted_iota(jnp.int32, (tile_cols, LANES), 0)
@@ -198,7 +225,7 @@
             jnp.broadcast_to(values[lower : lower + 1][:, None, :], thin),
         )
 
-    for block in range(channels // BLOCK):
+    for block in range(blocks):
         lanes = slice(block * BLOCK, (block + 1) * BLOCK)
         edges = dot(border_ref[...], patch_ref[:, lanes])
         inner = jnp.concatenate(
@@ -232,40 +259,45 @@
             total = total + dot(wide_ref[first : first + tokens, :], taps_ref[row_shift])
         summed_ref[:, lanes] = total
 
-    piece = 128
     inverse = 1.0 / channels
 
-    def normalise(step, _):
-        at = pl.ds(pl.multiple_of(step * piece, piece), piece)
+    def normalise(start, extent):
+        at = pl.ds(pl.multiple_of(start, extent), extent)
         values = summed_ref[at, :]
         centred = values - jnp.sum(values, axis=-1, keepdims=True) * inverse
         variance = jnp.sum(centred * centred, axis=-1, keepdims=True) * inverse
         features_ref[at, :] = (centred * lax.rsqrt(variance + 1e-05)).astype(BF16)
-        return 0
-
-    lax.fori_loop(0, tokens // piece, normalise, 0)
-    store = pltpu.make_async_copy(features_ref, features_hbm, load_sem.at[len(loads)])
-    store.start()
-    loads[7].wait()
-
-    def project(step, _):
-        for base in (0, channels):
-            at = pl.ds(pl.multiple_of(base + step * BLOCK, BLOCK), BLOCK)
-            found = dot(features_ref[...], kv_ref[:, at]).astype(BF16)
-            for inner in range(BLOCK // LANES):
-                pair = step * (BLOCK // LANES) + inner
-                mine = found[:, inner * LANES : (inner + 1) * LANES]
-                if base == 0:
-                    keys_ref[pair] = mine
-                else:
-                    mine = mine.T
-                    for which in range(2):
-                        turned_ref[pair, which, :head_dim, :] = mine[
-                            which * head_dim : (which + 1) * head_dim
-                        ]
-        return 0
-
-    lax.fori_loop(0, channels // BLOCK, project, 0)
+
+    def project(step, start, extent):
+        at = pl.ds(pl.multiple_of(step * BLOCK, BLOCK), BLOCK)
+        found = dot(features_ref[start : start + extent, :], kv_ref[:, at]).astype(BF16)
+        for inner in range(BLOCK // LANES):
+            keys_ref[step * (BLOCK // LANES) + inner, start : start + extent, :] = found[
+                :, inner * LANES : (inner + 1) * LANES
+            ]
+
+    first = tokens // 2
+    steps = 2 * channels // BLOCK
+    piece = first // steps
+
+    def begin(step, _):
+        normalise(step * LANES, LANES)
+        return 0
+
+    lax.fori_loop(0, first // LANES, begin, 0)
+    fetches["kv"].wait()
+
+    def middle(step, _):
+        project(step, 0, first)
+        normalise(first + step * piece, piece)
+        return 0
+
+    def last(step, _):
+        project(step, first, first)
+        return 0
+
+    lax.fori_loop(0, steps, middle, 0)
+    lax.fori_loop(0, steps, last, 0)
 
     lane = lax.broadcasted_iota(jnp.int32, (1, LANES), 1)
     low = lane < head_dim
@@ -288,16 +320,10 @@
         score_ref[which, at, :] = scores
         return jnp.maximum(peak, jnp.max(scores.reshape(chunk // 8, 8, latent_count), 0))
 
-    def weigh(pair, part, which, peak, total):
+    def weigh(part, which, peak, total):
         at = slice(part * chunk, (part + 1) * chunk)
         weights = jnp.exp2((score_ref[which, at, :] - peak) * gain).astype(BF16)
-        return total + dot(turned_ref[pair, which, :, at], weights)
-
-    def remote(source, target, send, recv, peer):
-        return pltpu.make_async_remote_copy(
-            src_ref=source, dst_ref=target, send_sem=send, recv_sem=recv,
-            device_id=peer, device_id_type=MESH,
-        )
+        return total + dot(turned_ref[which, :, at], weights)
 
     def to_twin(pair):
         return remote(
@@ -391,6 +417,12 @@
                 for copy in to_col(group, step):
                     copy.start()
 
+    def asked_wait(step, _):
+        share(step).wait_recv()
+        return 0
+
+    lax.fori_loop(0, mine_from, asked_wait, 0)
+    lax.fori_loop(mine_to, blocks, asked_wait, 0)
     peak = fresh
     queries = asked(0, 0)
     for part in range(2):
@@ -398,6 +430,9 @@
     peak_ref[...] = peak
 
     def step(pair, _):
+        turned = keys_ref[pairs + pair].T
+        for which in range(2):
+            turned_ref[which, :head_dim, :] = turned[which * head_dim : (which + 1) * head_dim]
         current = peak_ref[...]
         for which in range(2):
             following = pair if which == 0 else jnp.minimum(pair + 1, pairs - 1)
@@ -407,7 +442,7 @@
             peak = fresh
             for part in range(2):
                 peak = score(following, part, queries, 1 - which, peak)
-                total = weigh(pair, part, which, top, total)
+                total = weigh(part, which, top, total)
             line = lax.broadcasted_iota(jnp.int32, (8, latent_count), 0) == 0
             stat = jnp.where(line, top, total[head_dim : head_dim + 8])
             for half_at in range(2):
@@ -469,11 +504,16 @@
         return 0
 
     lax.fori_loop(0, pairs, drain, 0)
+
+    def asked_drain(step, _):
+        share(step).wait_send()
+        return 0
+
+    lax.fori_loop(mine_from, mine_to, asked_drain, 0)
     for group in range(groups):
         for step in range(1, half):
             for copy in to_col(group, step):
                 copy.wait_send()
-    store.wait()
     for number, (down, across, _, _) in enumerate(moves):
         @pl.when(inside(down, across))
         def _(number=number):
@@ -510,11 +550,11 @@
     return pl.pallas_call(
         functools.partial(slide, HEADS),
         out_shape=(
-            jax.ShapeDtypeStruct((tokens, channels), BF16),
-            jax.ShapeDtypeStruct((own, channels), BF16),
+            pltpu.VMEM((tokens, channels), BF16),
+            pltpu.VMEM((own, channels), BF16),
         ),
-        in_specs=[leave] * 7,
-        out_specs=(leave, pl.BlockSpec(memory_space=pltpu.VMEM)),
+        in_specs=[pl.BlockSpec(memory_space=pltpu.HBM)] * 7,
+        out_specs=(pl.BlockSpec(memory_space=pltpu.VMEM),) * 2,
         scratch_shapes=[
             like(array)
             for array in (pixels, tissue, patch_weight, conv_weight, kv_weight, query_weight)
@@ -527,10 +567,9 @@
             pltpu.VMEM(((tile_rows + 2) * tile_cols, 3 * BLOCK), BF16),
             pltpu.VMEM((3, 3 * BLOCK, BLOCK), BF16),
             pltpu.VMEM((tokens, channels), F32),
-            pltpu.VMEM((tokens, channels), BF16),
             pltpu.VMEM((latent_count, channels), BF16),
-            pltpu.VMEM((pairs, tokens, LANES), BF16),
-            pltpu.VMEM((pairs, 2, head_dim + CORNER, tokens), BF16),
+            pltpu.VMEM((2 * pairs, tokens, LANES), BF16),
+            pltpu.VMEM((2, head_dim + CORNER, tokens), BF16),
             pltpu.VMEM((tokens, LANES), BF16),
             pltpu.VMEM((tile_rows, LANES), F32),
             pltpu.VMEM((2, tokens, latent_count), F32),
@@ -543,69 +582,51 @@
         + [pltpu.VMEM((half, head_dim, LANES), F32), pltpu.VMEM((half, 8, LANES), F32)]
         + blocks(groups, half)
         + blocks(groups, half - 1)
-        + [pltpu.SemaphoreType.DMA((9,))]
+        + [pltpu.SemaphoreType.DMA((7,)), pltpu.SemaphoreType.DMA((channels // BLOCK,))]
+        + sems(channels // BLOCK)
         + sems(8)
         + sems(pairs)
         + sems(pairs, row_count - 1, 2)
         + sems(groups, half - 1, 2),
         compiler_params=pltpu.CompilerParams(
-            collective_id=1, has_side_effects=True, vmem_limit_bytes=60 * 1024 * 1024
+            collective_id=1, has_side_effects=True, vmem_limit_bytes=50 * 1024 * 1024
         ),
         name="slide",
-    )(pixels, tissue, patch_weight, conv_weight, kv_weight, query_weight, latents)
-
-
-def finish(
-    features_hbm, normed_ref, weight_hbm,
-    copied_hbm, out_ref,
-    features_ref, weight_ref, in_sem, out_sem, load_sem,
-):
-    parts = in_sem.shape[0]
-    extent = features_ref.shape[0] // parts
-    load = pltpu.make_async_copy(weight_hbm, weight_ref, load_sem)
-
-    def fetch(part):
-        at = pl.ds(part * extent, extent)
-        return pltpu.make_async_copy(features_hbm.at[at], features_ref.at[at], in_sem.at[part])
-
-    def store(part):
-        at = pl.ds(part * extent, extent)
-        return pltpu.make_async_copy(features_ref.at[at], copied_hbm.at[at], out_sem.at[part])
-
-    for part in range(parts):
-        fetch(part).start()
-    load.start()
-    for part in range(parts):
-        fetch(part).wait()
-        store(part).start()
-    load.wait()
+    )(
+        *(
+            pltpu.with_memory_space_constraint(array, pltpu.HBM)
+            for array in (
+                pixels, tissue, patch_weight, conv_weight, kv_weight, query_weight, latents
+            )
+        )
+    )
+
+
+def finish(features_ref, normed_ref, weight_ref, features_hbm, out_ref, sem):
+    store = pltpu.make_async_copy(features_ref, features_hbm, sem)
+    store.start()
     out_ref[...] = dot(normed_ref[...], weight_ref[...]).astype(BF16)
-    for part in range(parts):
-        store(part).wait()
+    store.wait()
 
 
 def place(features, normed, out_weight):
-    leave = pl.BlockSpec(memory_space=pl.ANY)
     vmem = pl.BlockSpec(memory_space=pltpu.VMEM)
-    parts = 4
     return pl.pallas_call(
         finish,
         out_shape=(
             jax.ShapeDtypeStruct(features.shape, BF16),
             jax.ShapeDtypeStruct((normed.shape[0], out_weight.shape[1]), BF16),
         ),
-        in_specs=[leave, vmem, leave],
-        out_specs=(leave, vmem),
-        scratch_shapes=[
-            pltpu.VMEM(features.shape, BF16),
-            pltpu.VMEM(out_weight.shape, BF16),
-            pltpu.SemaphoreType.DMA((parts,)),
-            pltpu.SemaphoreType.DMA((parts,)),
-            pltpu.SemaphoreType.DMA,
-        ],
-        compiler_params=pltpu.CompilerParams(vmem_limit_bytes=32 * 1024 * 1024),
+        in_specs=[vmem] * 3,
+        out_specs=(pl.BlockSpec(memory_space=pl.ANY), vmem),
+        scratch_shapes=[pltpu.SemaphoreType.DMA],
+        compiler_params=pltpu.CompilerParams(vmem_limit_bytes=24 * 1024 * 1024),
         name="place",
-    )(features, normed, out_weight)
+    )(
+        pltpu.with_memory_space_constraint(features, pltpu.VMEM),
+        pltpu.with_memory_space_constraint(normed, pltpu.VMEM),
+        pltpu.with_memory_space_constraint(out_weight, pltpu.VMEM),
+    )
 
 
 def shards(pixels, tissue, patch_weight, conv_weight, kv_weight, query_weight, out_weight, latents):

time: 53.8 us -> 51.4 us (0.955)
  local copies, waits for them, and re-layouts: 2.35 us -> 0.01 us
    unnamed x6 -> x2, local copies, waits for them, and re-layouts: 2.35 us -> 0.01 us
where the time goes in v3:
time: 51.4 us; the launch traced here: 51.3 us
  Pallas kernels  50.6 us (98%)
  between operations  0.66 us (1%)
    pallas_call x1, Pallas kernels, embed_attend(): pl.pallas_call(functools.partial(slide, HEADS), out_shape=(pltpu.VMEM((to...  48.6 us
    pallas_call x1, Pallas kernels, place(): pl.pallas_call(finish, out_shape=(jax.ShapeDtypeStruct(features.shape, BF...  2.03 us

profile of v3, /device:TPU:0, one launch (start us, length us, event | category | flops | bytes accessed | tf_op | source)
XLA Modules:
  0.0 51.3 jit_solution(2612215736992514710)
XLA Ops:
  0.6 0.0 copy-start
  0.6 48.6 %slide.1 = (bf16[1024,1024]{1,0:T(8,128)(2,1)S(1)}, bf16[16,1024]{1,0:T(8,128)(2,1)S(1)}) custom-call(bf16[32,32,768]{2,1,0:T(8,128)(2,1)} %pixels_hbm.1, s32[32,32]{1,0:T(8,128)} %tissue_hbm.1, bf16[768,1024]{1,0:T(8,128)(2,1)} %patch_hbm.1, bf16[9,32,1024]{2,1,0:T(8,128)(2,1)} %conv_hbm.1, bf16[1024,2048]{1,0:T(8,128)(2,1)} %kv_hbm.1, ...), custom_call_target="tpu_custom_call" | custom-call | tf_op jit(solution)/shard_map/slide/pallas_call | solution.py:550
  49.2 0.0 copy-done
  49.2 2.0 %place.1 = (bf16[1024,1024]{1,0:T(8,128)(2,1)}, bf16[16,1024]{1,0:T(8,128)(2,1)}) custom-call(bf16[1024,1024]{1,0:T(8,128)(2,1)S(1)} %get-tuple-element.6.features_ref, bf16[16,1024]{1,0:T(8,128)(2,1)S(1)} %get-tuple-element.7.normed_ref, bf16[1024,1024]{1,0:T(8,128)(2,1)S(1)} %copy-done), custom_call_target="tpu_custom_call" | custom-call | tf_op jit(solution)/shard_map/place/pallas_call | solution.py:614
Async XLA Ops:
  0.6 48.6 %copy-start = (bf16[1024,1024]{1,0:T(8,128)(2,1)S(1)}, bf16[1024,1024]{1,0:T(8,128)(2,1)}, u32[]{:S(2)}) copy-start(bf16[1024,1024]{1,0:T(8,128)(2,1)} %weight_ref.1) | copy-start | bytes 6291460

commit v4 on v3

--- a/solution.py
+++ b/solution.py
@@ -12,7 +12,7 @@
 LANES = 128
 PAD = 8
 CORNER = 16
-LAG = 4
+LAG = 6
 LOG2_E = 1.4426950408889634
 F32 = jnp.float32
 BF16 = jnp.bfloat16
@@ -42,7 +42,7 @@
     border_ref, side_ref, embedded_ref, wide_ref, taps_ref, summed_ref,
     query_ref, keys_ref, turned_ref, bias_ref, mask_ref, score_ref, peak_ref,
     part_ref, twin_ref, row_num, row_stat, got_num, got_stat,
-    build_num, build_stat, col_num, col_stat, end_num, end_stat,
+    build_num, build_stat, spread_ref, col_num, col_stat, end_num, end_stat,
     load_sem, patch_sem, ask_send, ask_recv, halo_send, halo_recv,
     twin_send, twin_recv, row_send, row_recv, col_send, col_recv,
 ):
@@ -171,7 +171,7 @@
     lax.fori_loop(0, blocks, embed, 0)
     for name in ("low", "high", "ask"):
         fetches[name].wait()
-    shared = blocks - blocks // 4
+    shared = blocks
     mine_from = jnp.where(side == 0, 0, shared)
     mine_to = jnp.where(side == 0, shared, blocks)
 
@@ -268,36 +268,22 @@
         variance = jnp.sum(centred * centred, axis=-1, keepdims=True) * inverse
         features_ref[at, :] = (centred * lax.rsqrt(variance + 1e-05)).astype(BF16)
 
-    def project(step, start, extent):
+    def project(step, _):
         at = pl.ds(pl.multiple_of(step * BLOCK, BLOCK), BLOCK)
-        found = dot(features_ref[start : start + extent, :], kv_ref[:, at]).astype(BF16)
+        found = dot(features_ref[...], kv_ref[:, at]).astype(BF16)
         for inner in range(BLOCK // LANES):
-            keys_ref[step * (BLOCK // LANES) + inner, start : start + extent, :] = found[
+            keys_ref[step * (BLOCK // LANES) + inner] = found[
                 :, inner * LANES : (inner + 1) * LANES
             ]
-
-    first = tokens // 2
-    steps = 2 * channels // BLOCK
-    piece = first // steps
+        return 0
 
     def begin(step, _):
         normalise(step * LANES, LANES)
         return 0
 
-    lax.fori_loop(0, first // LANES, begin, 0)
+    lax.fori_loop(0, tokens // LANES, begin, 0)
     fetches["kv"].wait()
-
-    def middle(step, _):
-        project(step, 0, first)
-        normalise(first + step * piece, piece)
-        return 0
-
-    def last(step, _):
-        project(step, first, first)
-        return 0
-
-    lax.fori_loop(0, steps, middle, 0)
-    lax.fori_loop(0, steps, last, 0)
+    lax.fori_loop(0, 2 * channels // BLOCK, project, 0)
 
     lane = lax.broadcasted_iota(jnp.int32, (1, LANES), 1)
     low = lane < head_dim
@@ -306,8 +292,23 @@
     chunk = tokens // 2
     fresh = jnp.full((8, latent_count), -3e38, F32)
 
+    def ordered(pair, which):
+        at = pl.ds(pl.multiple_of(pair * LANES, LANES), LANES)
+        turn = lax.rem(pair, per_group)
+        pieces = []
+        for line in range(2 * row_count):
+            start = (line if which == 0 else line ^ 1) * per_row
+            if own % CORNER == 0:
+                for place in range(half):
+                    source = start + lax.rem(place - turn + half, half) * own
+                    pieces.append(query_ref[pl.ds(pl.multiple_of(source, own), own), at])
+            else:
+                block = query_ref[start : start + per_row, at].astype(F32)
+                pieces.append(pltpu.roll(block, turn * own, 0).astype(BF16))
+        return jnp.concatenate(pieces, 0)
+
     def asked(pair, which):
-        queries = query_ref[:, pl.ds(pl.multiple_of(pair * LANES, LANES), LANES)]
+        queries = ordered(pair, which)
         mine = query_low if which == 0 else jnp.logical_not(query_low)
         return jnp.concatenate([jnp.where(mine, queries, jnp.zeros_like(queries)), ones], 1)
 
@@ -353,11 +354,11 @@
             for kind, (source, landing) in enumerate(((col_num, end_num), (col_stat, end_stat)))
         ]
 
-    first_line = lax.broadcasted_iota(jnp.int32, (8, LANES), 0) == 0
+    first_line = lax.broadcasted_iota(jnp.int32, (2, LANES), 0) == 0
+    region = lax.div(lax.rem(lane, per_row), own)
     extent = head_dim + 8
 
     def with_twin(pair):
-        to_twin(pair).wait_recv()
         merged = []
         for which in range(2):
             base = which * extent
@@ -369,24 +370,14 @@
         for target in range(row_count):
             tile = target * per_row // LANES
             at = slice(tile * LANES, (tile + 1) * LANES)
-
-            def joined(one, two, target=target, at=at):
-                one, two = one[:, at], two[:, at]
-                if target * per_row % LANES == 0:
-                    return jnp.where(low, one, pltpu.roll(two, per_row, 1))
-                return jnp.where(low, pltpu.roll(one, per_row, 1), two)
-
-            number, peak, total = [joined(one, two) for one, two in zip(*merged)]
+            begin, after = merged if target % 2 == 0 else merged[::-1]
+            number, peak, total = [
+                jnp.where(low, one[:, at], two[:, at]) for one, two in zip(begin, after)
+            ]
             row_num[pair, target] = number.astype(BF16)
             row_stat[pair, target] = jnp.where(first_line, peak, total)
-        for step in range(1, row_count):
-            for copy in to_row(pair, step):
-                copy.start()
 
     def with_rows(pair):
-        for step in range(1, row_count):
-            for copy in to_row(pair, step):
-                copy.wait_recv()
         items = []
         for values, stat in [(row_num[pair, row], row_stat[pair, row])] + [
             (got_num[pair, step], got_stat[pair, step]) for step in range(row_count - 1)
@@ -394,28 +385,28 @@
             items.append((values.astype(F32), stat[0:1], stat[1:2]))
         number, peak, total = merge(items, gain)
         stat = jnp.where(first_line, peak, total)
-        place = lax.rem(pair, per_group) * (2 * own)
+        turn = lax.rem(pair, per_group)
         for target in range(half):
-            for which in range(2):
-                begin = place + which * own
-                source = which * head_dim + target * own
-                shift = lax.rem(begin - source + LANES, LANES)
-                here = jnp.logical_and(lane >= begin, lane < begin + own)
-                build_num[target] = jnp.where(
-                    here, pltpu.roll(number, shift, 1), build_num[target]
-                )
-                build_stat[target] = jnp.where(
-                    here, pltpu.roll(stat, shift, 1), build_stat[target]
-                )
-
-        @pl.when(lax.rem(pair, per_group) == per_group - 1)
-        def _():
-            group = lax.div(pair, per_group)
-            col_num[group] = build_num[...].astype(BF16)
-            col_stat[group] = build_stat[...]
-            for step in range(1, half):
-                for copy in to_col(group, step):
-                    copy.start()
+            here = region == lax.rem(turn + target, half)
+            build_num[target] = jnp.where(here, number, build_num[target])
+            build_stat[target] = jnp.where(here, stat, build_stat[target])
+
+    def send_rows(pair):
+        for step in range(1, row_count):
+            for copy in to_row(pair, step):
+                copy.start()
+
+    def wait_rows(pair):
+        for step in range(1, row_count):
+            for copy in to_row(pair, step):
+                copy.wait_recv()
+
+    def send_cols(group):
+        col_num[group] = build_num[...].astype(BF16)
+        col_stat[group] = build_stat[...]
+        for step in range(1, half):
+            for copy in to_col(group, step):
+                copy.start()
 
     def asked_wait(step, _):
         share(step).wait_recv()
@@ -430,6 +421,14 @@
     peak_ref[...] = peak
 
     def step(pair, _):
+        @pl.when(pair >= 2)
+        def _():
+            to_twin(pair - 2).wait_recv()
+
+        @pl.when(pair >= LAG)
+        def _():
+            wait_rows(pair - LAG)
+
         turned = keys_ref[pairs + pair].T
         for which in range(2):
             turned_ref[which, :head_dim, :] = turned[which * head_dim : (which + 1) * head_dim]
@@ -437,6 +436,10 @@
         for which in range(2):
             following = pair if which == 0 else jnp.minimum(pair + 1, pairs - 1)
             queries = asked(following, 1 - which)
+            if which == 0:
+                with_twin(jnp.where(pair >= 2, pair - 2, pairs))
+            else:
+                with_rows(jnp.where(pair >= LAG, pair - LAG, pairs))
             top = jnp.max(current, 0, keepdims=True)
             total = jnp.zeros((head_dim + CORNER, latent_count), F32)
             peak = fresh
@@ -457,22 +460,33 @@
         peak_ref[...] = current
         to_twin(pair).start()
 
-        @pl.when(pair >= 1)
+        @pl.when(pair >= 2)
         def _():
-            with_twin(pair - 1)
-
-        @pl.when(pair >= LAG)
+            send_rows(pair - 2)
+
+        @pl.when(jnp.logical_and(pair >= LAG, lax.rem(pair - LAG, per_group) == per_group - 1))
         def _():
-            with_rows(pair - LAG)
-
-        return 0
+            send_cols(lax.div(pair - LAG, per_group))
+
+        return 0
+
+    def late_rows(pair):
+        wait_rows(pair)
+        with_rows(pair)
+        if pair % per_group == per_group - 1:
+            send_cols(pair // per_group)
 
     lax.fori_loop(0, pairs, step, 0)
-    for pair in range(pairs - LAG, pairs - 2):
-        with_rows(pair)
+    to_twin(pairs - 2).wait_recv()
+    with_twin(pairs - 2)
+    send_rows(pairs - 2)
+    for pair in range(pairs - LAG, pairs - 3):
+        late_rows(pair)
+    to_twin(pairs - 1).wait_recv()
     with_twin(pairs - 1)
-    for pair in range(pairs - 2, pairs):
-        with_rows(pair)
+    send_rows(pairs - 1)
+    for pair in range(pairs - 3, pairs):
+        late_rows(pair)
 
     pieces = []
     for group in range(groups):
@@ -485,12 +499,19 @@
         ]:
             items.append((values.astype(F32), stat[0:1], stat[1:2]))
         number, _, total = merge(items, gain)
-        tile = (number / total).T
-        for place in range(per_group):
-            base = place * 2 * own
-            pieces.append(
-                jnp.concatenate([tile[base : base + own], tile[base + own : base + 2 * own]], 1)
-            )
+        spread_ref[group] = (number / total).T
+    odd = lax.rem(row, 2)
+    for group in range(groups):
+        for turn in range(per_group):
+            place = lax.rem(slot + turn, half) * own
+            heads_here = []
+            for which in range(2):
+                begin = jnp.where(odd == which, 0, per_row) + place
+                if own % 8 == 0:
+                    heads_here.append(spread_ref[group, pl.ds(pl.multiple_of(begin, own), own), :])
+                else:
+                    heads_here.append(pltpu.roll(spread_ref[group], LANES - begin, 0)[:own])
+            pieces.append(jnp.concatenate(heads_here, 1))
     attended = jnp.concatenate(pieces, 1)
     mean = jnp.sum(attended * attended, axis=-1, keepdims=True) * (1.0 / channels)
     normed = (attended * lax.rsqrt(mean + 1e-06)).astype(BF16)
@@ -541,7 +562,7 @@
 
     def blocks(*extent):
         return [
-            pltpu.VMEM(extent + (head_dim, LANES), BF16), pltpu.VMEM(extent + (8, LANES), F32)
+            pltpu.VMEM(extent + (head_dim, LANES), BF16), pltpu.VMEM(extent + (2, LANES), F32)
         ]
 
     def sems(*extent):
@@ -574,12 +595,16 @@
             pltpu.VMEM((tile_rows, LANES), F32),
             pltpu.VMEM((2, tokens, latent_count), F32),
             pltpu.VMEM((8, latent_count), F32),
-            pltpu.VMEM((pairs, 2, 2 * (head_dim + 8), side_count), F32),
-            pltpu.VMEM((pairs, 2 * (head_dim + 8), side_count), F32),
+            pltpu.VMEM((pairs + 1, 2, 2 * (head_dim + 8), side_count), F32),
+            pltpu.VMEM((pairs + 1, 2 * (head_dim + 8), side_count), F32),
         ]
-        + blocks(pairs, row_count)
-        + blocks(pairs, row_count - 1)
-        + [pltpu.VMEM((half, head_dim, LANES), F32), pltpu.VMEM((half, 8, LANES), F32)]
+        + blocks(pairs + 1, row_count)
+        + blocks(pairs + 1, row_count - 1)
+        + [
+            pltpu.VMEM((half, head_dim, LANES), F32),
+            pltpu.VMEM((half, 2, LANES), F32),
+            pltpu.VMEM((groups, LANES, head_dim), F32),
+        ]
         + blocks(groups, half)
         + blocks(groups, half - 1)
         + [pltpu.SemaphoreType.DMA((7,)), pltpu.SemaphoreType.DMA((channels // BLOCK,))]

time: 51.4 us -> 49.8 us (0.969)
  Pallas kernels: 50.6 us -> 49 us
    pallas_call x1, Pallas kernels: 48.6 us -> 47 us  [embed_attend(): pl.pallas_call(functools.partial(slide, HEADS), out_shape=(pltpu.VMEM((to...]
where the time goes in v4:
time: 49.8 us; the launch traced here: 49.7 us
  Pallas kernels  49 us (98%)
  between operations  0.66 us (1%)
    pallas_call x1, Pallas kernels, embed_attend(): pl.pallas_call(functools.partial(slide, HEADS), out_shape=(pltpu.VMEM((to...  47 us
    pallas_call x1, Pallas kernels, place(): pl.pallas_call(finish, out_shape=(jax.ShapeDtypeStruct(features.shape, BF...  2.03 us

profile of v4, /device:TPU:0, one launch (start us, length us, event | category | flops | bytes accessed | tf_op | source)
XLA Modules:
  0.0 49.7 jit_solution(2051833048229964743)
XLA Ops:
  0.6 0.0 copy-start
  0.6 47.0 %slide.1 = (bf16[1024,1024]{1,0:T(8,128)(2,1)S(1)}, bf16[16,1024]{1,0:T(8,128)(2,1)S(1)}) custom-call(bf16[32,32,768]{2,1,0:T(8,128)(2,1)} %pixels_hbm.1, s32[32,32]{1,0:T(8,128)} %tissue_hbm.1, bf16[768,1024]{1,0:T(8,128)(2,1)} %patch_hbm.1, bf16[9,32,1024]{2,1,0:T(8,128)(2,1)} %conv_hbm.1, bf16[1024,2048]{1,0:T(8,128)(2,1)} %kv_hbm.1, ...), custom_call_target="tpu_custom_call" | custom-call | tf_op jit(solution)/shard_map/slide/pallas_call | solution.py:571
  47.6 0.0 copy-done
  47.6 2.0 %place.1 = (bf16[1024,1024]{1,0:T(8,128)(2,1)}, bf16[16,1024]{1,0:T(8,128)(2,1)}) custom-call(bf16[1024,1024]{1,0:T(8,128)(2,1)S(1)} %get-tuple-element.6.features_ref, bf16[16,1024]{1,0:T(8,128)(2,1)S(1)} %get-tuple-element.7.normed_ref, bf16[1024,1024]{1,0:T(8,128)(2,1)S(1)} %copy-done), custom_call_target="tpu_custom_call" | custom-call | tf_op jit(solution)/shard_map/place/pallas_call | solution.py:639
Async XLA Ops:
  0.6 47.0 %copy-start = (bf16[1024,1024]{1,0:T(8,128)(2,1)S(1)}, bf16[1024,1024]{1,0:T(8,128)(2,1)}, u32[]{:S(2)}) copy-start(bf16[1024,1024]{1,0:T(8,128)(2,1)} %weight_ref.1) | copy-start | bytes 6291460

commit v5 on v4

--- a/solution.py
+++ b/solution.py
@@ -241,23 +241,35 @@
         full = jnp.concatenate(
             [inner.reshape(rows_ext, tile_cols, BLOCK), flank], 1
         ).reshape(rows_ext * col_ext, BLOCK)
-        for col_shift, amount in ((0, 1), (2, rows_ext * col_ext - 1)):
-            moved = pltpu.roll(full, amount, 0).reshape(rows_ext, col_ext, BLOCK)
-            moved = moved[:, :tile_cols].reshape(rows_ext * tile_cols, BLOCK)
-            wide_ref[:, col_shift * BLOCK : (col_shift + 1) * BLOCK] = moved.astype(BF16)
-        wide_ref[:, BLOCK : 2 * BLOCK] = inner.astype(BF16)
-        for tap in range(9):
-            small = conv_ref[tap, :, lanes]
-            tiled = jnp.concatenate([small] * (BLOCK // group_width), 0)
-            row_shift, col_shift = tap // 3, tap % 3
-            taps_ref[row_shift, col_shift * BLOCK : (col_shift + 1) * BLOCK, :] = jnp.where(
-                same, tiled, jnp.zeros_like(tiled)
-            )
-        total = wide_ref[tile_cols : tile_cols + tokens, BLOCK : 2 * BLOCK].astype(F32)
-        for row_shift in range(3):
-            first = row_shift * tile_cols
-            total = total + dot(wide_ref[first : first + tokens, :], taps_ref[row_shift])
-        summed_ref[:, lanes] = total
+        for col_shift in range(3):
+            moved = inner
+            if col_shift != 1:
+                moved = pltpu.roll(full, 1 if col_shift == 0 else rows_ext * col_ext - 1, 0)
+                moved = moved.reshape(rows_ext, col_ext, BLOCK)[:, :tile_cols]
+            moved = moved.astype(BF16).reshape(rows_ext // 2, 2, tile_cols, BLOCK)
+            even, odd = moved[:, 0], moved[:, 1]
+            near, far, here, after = even[:-1], even[1:], odd[:-1], odd[1:]
+            if col_shift == 1:
+                centres = [here, far]
+            at = slice(col_shift * BLOCK, (col_shift + 1) * BLOCK)
+            for number, mixed in enumerate((near - far, here + far, far - here, here - after)):
+                wide_ref[number, :, at] = mixed.reshape(tokens // 2, BLOCK)
+            ends = [conv_ref[3 * line + col_shift, :, lanes].astype(F32) for line in range(3)]
+            outer = ends[0] + ends[2]
+            for number, small in enumerate(
+                (ends[0], (outer + ends[1]) * 0.5, (outer - ends[1]) * 0.5, ends[2])
+            ):
+                tiled = jnp.concatenate([small.astype(BF16)] * (BLOCK // group_width), 0)
+                taps_ref[number, at, :] = jnp.where(same, tiled, jnp.zeros_like(tiled))
+        parts = [dot(wide_ref[number], taps_ref[number]) for number in range(4)]
+        upper = (parts[1] + parts[2]) + parts[0]
+        lower = parts[1] - parts[2] - parts[3]
+        split = (tile_rows // 2, tile_cols, BLOCK)
+        both = [
+            half_rows.reshape(split) + centre.astype(F32)
+            for half_rows, centre in zip((upper, lower), centres)
+        ]
+        summed_ref[:, lanes] = jnp.stack(both, 1).reshape(tokens, BLOCK)
 
     inverse = 1.0 / channels
 
@@ -585,8 +597,8 @@
             pltpu.VMEM((borders, patch_in), BF16),
             pltpu.VMEM((2, tile_rows, patch_in), BF16),
             pltpu.VMEM((tokens, channels), F32),
-            pltpu.VMEM(((tile_rows + 2) * tile_cols, 3 * BLOCK), BF16),
-            pltpu.VMEM((3, 3 * BLOCK, BLOCK), BF16),
+            pltpu.VMEM((4, tokens // 2, 3 * BLOCK), BF16),
+            pltpu.VMEM((4, 3 * BLOCK, BLOCK), BF16),
             pltpu.VMEM((tokens, channels), F32),
             pltpu.VMEM((latent_count, channels), BF16),
             pltpu.VMEM((2 * pairs, tokens, LANES), BF16),

time: 49.8 us -> 48.9 us (0.982)
  Pallas kernels: 49 us -> 48.1 us
    pallas_call x1, Pallas kernels: 47 us -> 46.1 us  [embed_attend(): pl.pallas_call(functools.partial(slide, HEADS), out_shape=(pltpu.VMEM((to...]
where the time goes in v5:
time: 48.9 us; the launch traced here: 48.7 us
  Pallas kernels  48.1 us (98%)
  between operations  0.66 us (1%)
    pallas_call x1, Pallas kernels, embed_attend(): pl.pallas_call(functools.partial(slide, HEADS), out_shape=(pltpu.VMEM((to...  46.1 us
    pallas_call x1, Pallas kernels, place(): pl.pallas_call(finish, out_shape=(jax.ShapeDtypeStruct(features.shape, BF...  2.03 us

profile of v5, /device:TPU:0, one launch (start us, length us, event | category | flops | bytes accessed | tf_op | source)
XLA Modules:
  0.0 48.7 jit_solution(12914493627754116423)
XLA Ops:
  0.6 0.0 copy-start
  0.6 46.1 %slide.1 = (bf16[1024,1024]{1,0:T(8,128)(2,1)S(1)}, bf16[16,1024]{1,0:T(8,128)(2,1)S(1)}) custom-call(bf16[32,32,768]{2,1,0:T(8,128)(2,1)} %pixels_hbm.1, s32[32,32]{1,0:T(8,128)} %tissue_hbm.1, bf16[768,1024]{1,0:T(8,128)(2,1)} %patch_hbm.1, bf16[9,32,1024]{2,1,0:T(8,128)(2,1)} %conv_hbm.1, bf16[1024,2048]{1,0:T(8,128)(2,1)} %kv_hbm.1, ...), custom_call_target="tpu_custom_call" | custom-call | tf_op jit(solution)/shard_map/slide/pallas_call | solution.py:583
  46.7 0.0 copy-done
  46.7 2.0 %place.1 = (bf16[1024,1024]{1,0:T(8,128)(2,1)}, bf16[16,1024]{1,0:T(8,128)(2,1)}) custom-call(bf16[1024,1024]{1,0:T(8,128)(2,1)S(1)} %get-tuple-element.6.features_ref, bf16[16,1024]{1,0:T(8,128)(2,1)S(1)} %get-tuple-element.7.normed_ref, bf16[1024,1024]{1,0:T(8,128)(2,1)S(1)} %copy-done), custom_call_target="tpu_custom_call" | custom-call | tf_op jit(solution)/shard_map/place/pallas_call | solution.py:651
Async XLA Ops:
  0.6 46.1 %copy-start = (bf16[1024,1024]{1,0:T(8,128)(2,1)S(1)}, bf16[1024,1024]{1,0:T(8,128)(2,1)}, u32[]{:S(2)}) copy-start(bf16[1024,1024]{1,0:T(8,128)(2,1)} %weight_ref.1) | copy-start | bytes 6291460

commit v6 on v5

--- a/solution.py
+++ b/solution.py
@@ -13,6 +13,7 @@
 PAD = 8
 CORNER = 16
 LAG = 6
+PIECE = 32
 LOG2_E = 1.4426950408889634
 F32 = jnp.float32
 BF16 = jnp.bfloat16
@@ -86,6 +87,7 @@
             patch_hbm.at[:, at], patch_ref.at[:, at], patch_sem.at[step]
         )
 
+    fetches["tissue"].start()
     fetches["pixels"].start()
     for block in range(blocks):
         patch_load(block).start()
@@ -151,46 +153,7 @@
         @pl.when(inside(*moves[number][:2]))
         def _(number=number):
             shift(number).start()
-    fetches["pixels"].wait()
-    side_ref[0] = pixels_ref[:, 0, :]
-    side_ref[1] = pixels_ref[:, tile_cols - 1, :]
-    for number in range(6, 8):
-        @pl.when(inside(*moves[number][:2]))
-        def _(number=number):
-            shift(number).start()
-    for name in ("low", "high", "ask", "conv", "tissue", "kv"):
-        fetches[name].start()
-
-    def embed(step, _):
-        at = pl.ds(pl.multiple_of(step * BLOCK, BLOCK), BLOCK)
-        patch_load(step).wait()
-        pixels = pixels_ref[...].reshape(tokens, patch_in)
-        embedded_ref[:, at] = dot(pixels, patch_ref[:, at])
-        return 0
-
-    lax.fori_loop(0, blocks, embed, 0)
-    for name in ("low", "high", "ask"):
-        fetches[name].wait()
-    shared = blocks
-    mine_from = jnp.where(side == 0, 0, shared)
-    mine_to = jnp.where(side == 0, shared, blocks)
-
-    def share(step):
-        at = pl.ds(pl.multiple_of(step * BLOCK, BLOCK), BLOCK)
-        return remote(
-            query_ref.at[:, at], query_ref.at[:, at], ask_send.at[step], ask_recv.at[step], twin
-        )
-
-    def ask(step, _):
-        at = pl.ds(pl.multiple_of(step * BLOCK, BLOCK), BLOCK)
-        latents = latent_ref[...].reshape(latent_count, ask_ref.shape[0])
-        query_ref[:, at] = dot(latents, ask_ref[:, at]).astype(BF16)
-        share(step).start()
-        return 0
-
-    lax.fori_loop(mine_from, mine_to, ask, 0)
-    for name in ("conv", "tissue"):
-        fetches[name].wait()
+    fetches["tissue"].wait()
     mask_ref[...] = jnp.zeros_like(mask_ref)
     mask_ref[:, :tile_cols] = jnp.where(tissue_ref[...] > 0, 0.0, LOW)
     spot = lax.broadcasted_iota(jnp.int32, (tile_cols, LANES), 0)
@@ -200,6 +163,45 @@
         bias_ref[tile_row * tile_cols : (tile_row + 1) * tile_cols, :] = jnp.where(
             spot, line, 0.0
         ).astype(BF16)
+    fetches["pixels"].wait()
+    side_ref[0] = pixels_ref[:, 0, :]
+    side_ref[1] = pixels_ref[:, tile_cols - 1, :]
+    for number in range(6, 8):
+        @pl.when(inside(*moves[number][:2]))
+        def _(number=number):
+            shift(number).start()
+    for name in ("low", "high", "ask", "conv", "kv"):
+        fetches[name].start()
+
+    def embed(step, _):
+        at = pl.ds(pl.multiple_of(step * BLOCK, BLOCK), BLOCK)
+        patch_load(step).wait()
+        pixels = pixels_ref[...].reshape(tokens, patch_in)
+        embedded_ref[:, at] = dot(pixels, patch_ref[:, at])
+        return 0
+
+    lax.fori_loop(0, blocks, embed, 0)
+    for name in ("low", "high", "ask"):
+        fetches[name].wait()
+    shared = blocks
+    mine_from = jnp.where(side == 0, 0, shared)
+    mine_to = jnp.where(side == 0, shared, blocks)
+
+    def share(step):
+        at = pl.ds(pl.multiple_of(step * BLOCK, BLOCK), BLOCK)
+        return remote(
+            query_ref.at[:, at], query_ref.at[:, at], ask_send.at[step], ask_recv.at[step], twin
+        )
+
+    def ask(step, _):
+        at = pl.ds(pl.multiple_of(step * BLOCK, BLOCK), BLOCK)
+        latents = latent_ref[...].reshape(latent_count, ask_ref.shape[0])
+        query_ref[:, at] = dot(latents, ask_ref[:, at]).astype(BF16)
+        share(step).start()
+        return 0
+
+    lax.fori_loop(mine_from, mine_to, ask, 0)
+    fetches["conv"].wait()
     for number, (down, across, _, target) in enumerate(moves):
         @pl.when(inside(-down, -across))
         def _(number=number):
@@ -273,12 +275,14 @@
 
     inverse = 1.0 / channels
 
-    def normalise(start, extent):
-        at = pl.ds(pl.multiple_of(start, extent), extent)
-        values = summed_ref[at, :]
-        centred = values - jnp.sum(values, axis=-1, keepdims=True) * inverse
-        variance = jnp.sum(centred * centred, axis=-1, keepdims=True) * inverse
-        features_ref[at, :] = (centred * lax.rsqrt(variance + 1e-05)).astype(BF16)
+    def normalise(step, _):
+        for part in range(LANES // PIECE):
+            at = pl.ds(pl.multiple_of(step * LANES + part * PIECE, PIECE), PIECE)
+            values = summed_ref[at, :]
+            centred = values - jnp.sum(values, axis=-1, keepdims=True) * inverse
+            variance = jnp.sum(centred * centred, axis=-1, keepdims=True) * inverse
+            features_ref[at, :] = (centred * lax.rsqrt(variance + 1e-05)).astype(BF16)
+        return 0
 
     def project(step, _):
         at = pl.ds(pl.multiple_of(step * BLOCK, BLOCK), BLOCK)
@@ -289,11 +293,7 @@
             ]
         return 0
 
-    def begin(step, _):
-        normalise(step * LANES, LANES)
-        return 0
-
-    lax.fori_loop(0, tokens // LANES, begin, 0)
+    lax.fori_loop(0, tokens // LANES, normalise, 0)
     fetches["kv"].wait()
     lax.fori_loop(0, 2 * channels // BLOCK, project, 0)
 
@@ -432,22 +432,16 @@
         peak = score(0, part, queries, 0, peak)
     peak_ref[...] = peak
 
-    def step(pair, _):
-        @pl.when(pair >= 2)
-        def _():
-            to_twin(pair - 2).wait_recv()
-
-        @pl.when(pair >= LAG)
-        def _():
-            wait_rows(pair - LAG)
-
+    def attend(pair, final):
         turned = keys_ref[pairs + pair].T
         for which in range(2):
             turned_ref[which, :head_dim, :] = turned[which * head_dim : (which + 1) * head_dim]
         current = peak_ref[...]
         for which in range(2):
-            following = pair if which == 0 else jnp.minimum(pair + 1, pairs - 1)
-            queries = asked(following, 1 - which)
+            following = pair if which == 0 else pair + 1
+            ahead = not (final and which == 1)
+            if ahead:
+                queries = asked(following, 1 - which)
             if which == 0:
                 with_twin(jnp.where(pair >= 2, pair - 2, pairs))
             else:
@@ -456,7 +450,8 @@
             total = jnp.zeros((head_dim + CORNER, latent_count), F32)
             peak = fresh
             for part in range(2):
-                peak = score(following, part, queries, 1 - which, peak)
+                if ahead:
+                    peak = score(following, part, queries, 1 - which, peak)
                 total = weigh(part, which, top, total)
             line = lax.broadcasted_iota(jnp.int32, (8, latent_count), 0) == 0
             stat = jnp.where(line, top, total[head_dim : head_dim + 8])
@@ -472,6 +467,17 @@
         peak_ref[...] = current
         to_twin(pair).start()
 
+    def step(pair, _):
+        @pl.when(pair >= 2)
+        def _():
+            to_twin(pair - 2).wait_recv()
+
+        @pl.when(pair >= LAG)
+        def _():
+            wait_rows(pair - LAG)
+
+        attend(pair, False)
+
         @pl.when(pair >= 2)
         def _():
             send_rows(pair - 2)
@@ -488,7 +494,11 @@
         if pair % per_group == per_group - 1:
             send_cols(pair // per_group)
 
-    lax.fori_loop(0, pairs, step, 0)
+    lax.fori_loop(0, pairs - 1, step, 0)
+    to_twin(pairs - 3).wait_recv()
+    wait_rows(pairs - 1 - LAG)
+    attend(pairs - 1, True)
+    send_rows(pairs - 3)
     to_twin(pairs - 2).wait_recv()
     with_twin(pairs - 2)
     send_rows(pairs - 2)
@@ -500,6 +510,24 @@
     for pair in range(pairs - 3, pairs):
         late_rows(pair)
 
+    def drain(pair, _):
+        to_twin(pair).wait_send()
+        for step in range(1, row_count):
+            for copy in to_row(pair, step):
+                copy.wait_send()
+        return 0
+
+    lax.fori_loop(0, pairs, drain, 0)
+
+    def asked_drain(step, _):
+        share(step).wait_send()
+        return 0
+
+    lax.fori_loop(mine_from, mine_to, asked_drain, 0)
+    for number, (down, across, _, _) in enumerate(moves):
+        @pl.when(inside(down, across))
+        def _(number=number):
+            shift(number).wait_send()
     pieces = []
     for group in range(groups):
         items = []
@@ -529,28 +557,10 @@
     normed = (attended * lax.rsqrt(mean + 1e-06)).astype(BF16)
     normed_ref[...] = normed
 
-    def drain(pair, _):
-        to_twin(pair).wait_send()
-        for step in range(1, row_count):
-            for copy in to_row(pair, step):
-                copy.wait_send()
-        return 0
-
-    lax.fori_loop(0, pairs, drain, 0)
-
-    def asked_drain(step, _):
-        share(step).wait_send()
-        return 0
-
-    lax.fori_loop(mine_from, mine_to, asked_drain, 0)
     for group in range(groups):
         for step in range(1, half):
             for copy in to_col(group, step):
                 copy.wait_send()
-    for number, (down, across, _, _) in enumerate(moves):
-        @pl.when(inside(down, across))
-        def _(number=number):
-            shift(number).wait_send()
 
 
 def embed_attend(pixels, tissue, patch_weight, conv_weight, kv_weight, query_weight, latents):

time: 48.9 us -> 48.7 us (level)
  no operation moved by 1% of the time
where the time goes in v6:
time: 48.7 us; the launch traced here: 48.5 us
  Pallas kernels  47.9 us (98%)
  between operations  0.66 us (1%)
    pallas_call x1, Pallas kernels, embed_attend(): pl.pallas_call(functools.partial(slide, HEADS), out_shape=(pltpu.VMEM((to...  45.8 us
    pallas_call x1, Pallas kernels, place(): pl.pallas_call(finish, out_shape=(jax.ShapeDtypeStruct(features.shape, BF...  2.03 us

profile of v6, /device:TPU:0, one launch (start us, length us, event | category | flops | bytes accessed | tf_op | source)
XLA Modules:
  0.0 48.5 jit_solution(8091173497807555651)
XLA Ops:
  0.6 0.0 copy-start
  0.6 45.8 %slide.1 = (bf16[1024,1024]{1,0:T(8,128)(2,1)S(1)}, bf16[16,1024]{1,0:T(8,128)(2,1)S(1)}) custom-call(bf16[32,32,768]{2,1,0:T(8,128)(2,1)} %pixels_hbm.1, s32[32,32]{1,0:T(8,128)} %tissue_hbm.1, bf16[768,1024]{1,0:T(8,128)(2,1)} %patch_hbm.1, bf16[9,32,1024]{2,1,0:T(8,128)(2,1)} %conv_hbm.1, bf16[1024,2048]{1,0:T(8,128)(2,1)} %kv_hbm.1, ...), custom_call_target="tpu_custom_call" | custom-call | tf_op jit(solution)/shard_map/slide/pallas_call | solution.py:593
  46.5 0.0 copy-done
  46.5 2.0 %place.1 = (bf16[1024,1024]{1,0:T(8,128)(2,1)}, bf16[16,1024]{1,0:T(8,128)(2,1)}) custom-call(bf16[1024,1024]{1,0:T(8,128)(2,1)S(1)} %get-tuple-element.6.features_ref, bf16[16,1024]{1,0:T(8,128)(2,1)S(1)} %get-tuple-element.7.normed_ref, bf16[1024,1024]{1,0:T(8,128)(2,1)S(1)} %copy-done), custom_call_target="tpu_custom_call" | custom-call | tf_op jit(solution)/shard_map/place/pallas_call | solution.py:661
Async XLA Ops:
  0.6 45.8 %copy-start = (bf16[1024,1024]{1,0:T(8,128)(2,1)S(1)}, bf16[1024,1024]{1,0:T(8,128)(2,1)}, u32[]{:S(2)}) copy-start(bf16[1024,1024]{1,0:T(8,128)(2,1)} %weight_ref.1) | copy-start | bytes 6291460

commit v7 on v6

--- a/solution.py
+++ b/solution.py
@@ -37,8 +37,8 @@
 
 def slide(
     heads,
-    pixels_hbm, tissue_hbm, patch_hbm, conv_hbm, kv_hbm, ask_hbm, latent_hbm,
-    features_ref, normed_ref,
+    pixels_hbm, tissue_hbm, patch_hbm, conv_hbm, kv_hbm, ask_hbm, latent_hbm, last_hbm,
+    features_ref, normed_ref, last_ref,
     pixels_ref, tissue_ref, patch_ref, conv_ref, kv_ref, ask_ref, latent_ref,
     border_ref, side_ref, embedded_ref, wide_ref, taps_ref, summed_ref,
     query_ref, keys_ref, turned_ref, bias_ref, mask_ref, score_ref, peak_ref,
@@ -76,6 +76,7 @@
                 ("high", latent_hbm.at[:, :, 1], latent_ref.at[1]),
                 ("ask", ask_hbm, ask_ref), ("conv", conv_hbm, conv_ref),
                 ("tissue", tissue_hbm, tissue_ref), ("kv", kv_hbm, kv_ref),
+                ("last", last_hbm, last_ref),
             )
         )
     }
@@ -170,7 +171,7 @@
         @pl.when(inside(*moves[number][:2]))
         def _(number=number):
             shift(number).start()
-    for name in ("low", "high", "ask", "conv", "kv"):
+    for name in ("low", "high", "ask", "conv", "kv", "last"):
         fetches[name].start()
 
     def embed(step, _):
@@ -528,6 +529,7 @@
         @pl.when(inside(down, across))
         def _(number=number):
             shift(number).wait_send()
+    fetches["last"].wait()
     pieces = []
     for group in range(groups):
         items = []
@@ -563,7 +565,9 @@
                 copy.wait_send()
 
 
-def embed_attend(pixels, tissue, patch_weight, conv_weight, kv_weight, query_weight, latents):
+def embed_attend(
+    pixels, tissue, patch_weight, conv_weight, kv_weight, query_weight, latents, out_weight
+):
     tile_rows, tile_cols, patch_in = pixels.shape
     tokens = tile_rows * tile_cols
     row_count, col_count = lax.axis_size("rows"), lax.axis_size("cols")
@@ -595,9 +599,10 @@
         out_shape=(
             pltpu.VMEM((tokens, channels), BF16),
             pltpu.VMEM((own, channels), BF16),
+            pltpu.VMEM(out_weight.shape, BF16),
         ),
-        in_specs=[pl.BlockSpec(memory_space=pltpu.HBM)] * 7,
-        out_specs=(pl.BlockSpec(memory_space=pltpu.VMEM),) * 2,
+        in_specs=[pl.BlockSpec(memory_space=pltpu.HBM)] * 8,
+        out_specs=(pl.BlockSpec(memory_space=pltpu.VMEM),) * 3,
         scratch_shapes=[
             like(array)
             for array in (pixels, tissue, patch_weight, conv_weight, kv_weight, query_weight)
@@ -629,7 +634,7 @@
         ]
         + blocks(groups, half)
         + blocks(groups, half - 1)
-        + [pltpu.SemaphoreType.DMA((7,)), pltpu.SemaphoreType.DMA((channels // BLOCK,))]
+        + [pltpu.SemaphoreType.DMA((8,)), pltpu.SemaphoreType.DMA((channels // BLOCK,))]
         + sems(channels // BLOCK)
         + sems(8)
         + sems(pairs)
@@ -643,16 +648,20 @@
         *(
             pltpu.with_memory_space_constraint(array, pltpu.HBM)
             for array in (
-                pixels, tissue, patch_weight, conv_weight, kv_weight, query_weight, latents
+                pixels, tissue, patch_weight, conv_weight, kv_weight, query_weight, latents,
+                out_weight,
             )
         )
     )
 
 
-def finish(features_ref, normed_ref, weight_ref, features_hbm, out_ref, sem):
-    store = pltpu.make_async_copy(features_ref, features_hbm, sem)
+def finish(features_ref, normed_ref, weight_ref, features_hbm, out_hbm, out_ref, sem):
+    store = pltpu.make_async_copy(features_ref, features_hbm, sem.at[0])
     store.start()
     out_ref[...] = dot(normed_ref[...], weight_ref[...]).astype(BF16)
+    last = pltpu.make_async_copy(out_ref, out_hbm, sem.at[1])
+    last.start()
+    last.wait()
     store.wait()
 
 
@@ -665,8 +674,11 @@
             jax.ShapeDtypeStruct((normed.shape[0], out_weight.shape[1]), BF16),
         ),
         in_specs=[vmem] * 3,
-        out_specs=(pl.BlockSpec(memory_space=pl.ANY), vmem),
-        scratch_shapes=[pltpu.SemaphoreType.DMA],
+        out_specs=(pl.BlockSpec(memory_space=pl.ANY),) * 2,
+        scratch_shapes=[
+            pltpu.VMEM((normed.shape[0], out_weight.shape[1]), BF16),
+            pltpu.SemaphoreType.DMA((2,)),
+        ],
         compiler_params=pltpu.CompilerParams(vmem_limit_bytes=24 * 1024 * 1024),
         name="place",
     )(
@@ -678,8 +690,8 @@
 
 def shards(pixels, tissue, patch_weight, conv_weight, kv_weight, query_weight, out_weight, latents):
     tile_rows, tile_cols, _ = pixels.shape
-    features, normed = embed_attend(
-        pixels, tissue, patch_weight, conv_weight, kv_weight, query_weight, latents
+    features, normed, out_weight = embed_attend(
+        pixels, tissue, patch_weight, conv_weight, kv_weight, query_weight, latents, out_weight
     )
     features, latents_out = place(features, normed, out_weight)
     return (features.reshape(tile_rows, tile_cols, features.shape[1]), latents_out)

time: 48.7 us -> 48 us (0.986)
  Pallas kernels: 47.9 us -> 47.3 us
    pallas_call x1, Pallas kernels: 2.03 us -> 1.43 us  [place(): pl.pallas_call(finish, out_shape=(jax.ShapeDtypeStruct(features.shape, BF...]
where the time goes in v7:
time: 48 us; the launch traced here: 47.9 us
  Pallas kernels  47.3 us (99%)
  between operations  0.64 us (1%)
    pallas_call x1, Pallas kernels, embed_attend(): pl.pallas_call(functools.partial(slide, HEADS), out_shape=(pltpu.VMEM((to...  45.8 us
    pallas_call x1, Pallas kernels, place(): pl.pallas_call(finish, out_shape=(jax.ShapeDtypeStruct(features.shape, BF...  1.43 us

profile of v7, /device:TPU:0, one launch (start us, length us, event | category | flops | bytes accessed | tf_op | source)
XLA Modules:
  0.0 47.9 jit_solution(13911862723954771768)
XLA Ops:
  0.6 45.8 %slide.1 = (bf16[1024,1024]{1,0:T(8,128)(2,1)S(1)}, bf16[16,1024]{1,0:T(8,128)(2,1)S(1)}, bf16[1024,1024]{1,0:T(8,128)(2,1)S(1)}) custom-call(bf16[32,32,768]{2,1,0:T(8,128)(2,1)} %pixels_hbm.1, s32[32,32]{1,0:T(8,128)} %tissue_hbm.1, bf16[768,1024]{1,0:T(8,128)(2,1)} %patch_hbm.1, bf16[9,32,1024]{2,1,0:T(8,128)(2,1)} %conv_hbm.1, ...), custom_call_target="tpu_custom_call" | custom-call | tf_op jit(solution)/shard_map/slide/pallas_call | solution.py:597
  46.5 1.4 %place.1 = (bf16[1024,1024]{1,0:T(8,128)(2,1)}, bf16[16,1024]{1,0:T(8,128)(2,1)}) custom-call(bf16[1024,1024]{1,0:T(8,128)(2,1)S(1)} %get-tuple-element.7.features_ref, bf16[16,1024]{1,0:T(8,128)(2,1)S(1)} %get-tuple-element.8.normed_ref, bf16[1024,1024]{1,0:T(8,128)(2,1)S(1)} %get-tuple-element.9.weight_ref), custom_call_target="tpu_custom_call" | custom-call | tf_op jit(solution)/shard_map/place/pallas_call | solution.py:670

commit v8 on v7

--- a/solution.py
+++ b/solution.py
@@ -181,7 +181,7 @@
         embedded_ref[:, at] = dot(pixels, patch_ref[:, at])
         return 0
 
-    lax.fori_loop(0, blocks, embed, 0)
+    lax.fori_loop(0, blocks, embed, 0, unroll=4)
     for name in ("low", "high", "ask"):
         fetches[name].wait()
     shared = blocks
@@ -294,9 +294,9 @@
             ]
         return 0
 
-    lax.fori_loop(0, tokens // LANES, normalise, 0)
+    lax.fori_loop(0, tokens // LANES, normalise, 0, unroll=4)
     fetches["kv"].wait()
-    lax.fori_loop(0, 2 * channels // BLOCK, project, 0)
+    lax.fori_loop(0, 2 * channels // BLOCK, project, 0, unroll=4)
 
     lane = lax.broadcasted_iota(jnp.int32, (1, LANES), 1)
     low = lane < head_dim

time: 48 us -> 46.8 us (0.975)
  Pallas kernels: 47.3 us -> 45.8 us
    pallas_call x1, Pallas kernels: 45.8 us -> 44.4 us  [embed_attend(): pl.pallas_call(functools.partial(slide, HEADS), out_shape=(pltpu.VMEM((to...]
where the time goes in v8:
time: 46.8 us; the launch traced here: 46.6 us
  Pallas kernels  45.8 us (98%)
  between operations  0.8 us (2%)
    pallas_call x1, Pallas kernels, embed_attend(): pl.pallas_call(functools.partial(slide, HEADS), out_shape=(pltpu.VMEM((to...  44.4 us
    pallas_call x1, Pallas kernels, place(): pl.pallas_call(finish, out_shape=(jax.ShapeDtypeStruct(features.shape, BF...  1.43 us

profile of v8, /device:TPU:0, one launch (start us, length us, event | category | flops | bytes accessed | tf_op | source)
XLA Modules:
  0.0 46.6 jit_solution(3034068861534499463)
XLA Ops:
  0.6 44.4 %slide.1 = (bf16[1024,1024]{1,0:T(8,128)(2,1)S(1)}, bf16[16,1024]{1,0:T(8,128)(2,1)S(1)}, bf16[1024,1024]{1,0:T(8,128)(2,1)S(1)}) custom-call(bf16[32,32,768]{2,1,0:T(8,128)(2,1)} %pixels_hbm.1, s32[32,32]{1,0:T(8,128)} %tissue_hbm.1, bf16[768,1024]{1,0:T(8,128)(2,1)} %patch_hbm.1, bf16[9,32,1024]{2,1,0:T(8,128)(2,1)} %conv_hbm.1, ...), custom_call_target="tpu_custom_call" | custom-call | tf_op jit(solution)/shard_map/slide/pallas_call | solution.py:597
  45.0 1.4 %place.1 = (bf16[1024,1024]{1,0:T(8,128)(2,1)}, bf16[16,1024]{1,0:T(8,128)(2,1)}) custom-call(bf16[1024,1024]{1,0:T(8,128)(2,1)S(1)} %get-tuple-element.7.features_ref, bf16[16,1024]{1,0:T(8,128)(2,1)S(1)} %get-tuple-element.8.normed_ref, bf16[1024,1024]{1,0:T(8,128)(2,1)S(1)} %get-tuple-element.9.weight_ref), custom_call_target="tpu_custom_call" | custom-call | tf_op jit(solution)/shard_map/place/pallas_call | solution.py:670
